TPU v7x, 32 devices: a whole 2x2x4 slice. The times are simulated.
32 devices in a mesh: ctx: 8 (over z, y), wsh: 4 (over x, core).
Axes of the slice: x: 2, y: 2, z: 4, core: 2. Of those that a mesh axis runs over, the one named last changes fastest.
Arguments:
- tokens: bfloat16 [8, 1024, 1024], P('wsh', 'ctx'), may hold values from -6 to 6
- routes: int32 [8, 1024, 8], P('wsh', 'ctx'), may hold values from 0 to 31, all different within a row; in each aligned block of 128 rows (0 to 127, 128 to 255, ..., all dimensions but the last counted through in order) at most 48 rows name the same one
- in_weight: bfloat16 [1024, 2048], replicated, may hold values from -0.1875 to 0.1875
- out_weight: bfloat16 [1024, 1024], replicated, may hold values from -0.75 to 0.75
- first_gain: float32 [1024], replicated, may hold values from 0.5 to 1.5
- second_gain: float32 [1024], replicated, may hold values from 0.5 to 1.5
- router_weight: bfloat16 [1024, 32], replicated, may hold values from -0.1875 to 0.1875
- gate_weight: bfloat16 [32, 1024, 512], P('ctx', None, 'wsh'), may hold values from -0.1875 to 0.1875
- up_weight: bfloat16 [32, 1024, 512], P('ctx', None, 'wsh'), may hold values from -0.1875 to 0.1875
- down_weight: bfloat16 [32, 512, 1024], P('ctx', 'wsh'), may hold values from -0.75 to 0.75
- cotangent: bfloat16 [8, 1024, 1024], P('wsh', 'ctx'), may hold values from -6 to 6
Outputs:
- layer_out: bfloat16 [8, 1024, 1024], P('wsh', 'ctx')
- tokens_grad: bfloat16 [8, 1024, 1024], P('wsh', 'ctx')
- in_grad: float32 [1024, 2048], P(('ctx', 'wsh'))
- out_grad: float32 [1024, 1024], P(('ctx', 'wsh'))
- first_gain_grad: float32 [1024], P(('ctx', 'wsh'))
- second_gain_grad: float32 [1024], P(('ctx', 'wsh'))
- router_grad: float32 [1024, 32], P(('ctx', 'wsh'))
- gate_grad: float32 [32, 1024, 512], P('ctx', None, 'wsh')
- up_grad: float32 [32, 1024, 512], P('ctx', None, 'wsh')
- down_grad: float32 [32, 512, 1024], P('ctx', 'wsh')
Inputs may be any that keep to these rules, and one draw needn't show every extreme that they name: `routes`: in each aligned block of 128 rows (one sequence's rows on one index of ctx) the 8 experts of a row differ, and no expert is named by more than 48 rows of the block; some block reaches 48.
All inputs are finite; a program needn't handle non-finite values.
Results may differ from a plain program's by a relative error of at most 0.018.
Values may be sent and summed in bfloat16 or wider, within the bound.
No kernel may reach another device: no remote copies, remote signals or barrier semaphores. Data moves between devices by JAX's collectives and lax.ppermute only.
A program may use at most 256 MiB of HBM per device.

v0:
```python
import jax
import jax.numpy as jnp
from jax import lax
from jax.experimental import pallas as pl
from jax.experimental.pallas import tpu as pltpu
from jax.sharding import PartitionSpec as P

D = 1024
HEADS = 16
KV_HEADS = 8
HEAD_DIM = 64
EXPERTS = 32
TOP = 8
SEQ_TOK = 128
SEQ_GRP = 2
HALF = 64
MOST = 48


EPS = 1e-05
THETA = 10000.0
NEG = -1e30


def dealt(rows, length):
    owner = rows // SEQ_TOK
    offset = rows % SEQ_TOK
    early = owner * HALF + offset
    late = length - (owner + 1) * HALF + offset - HALF
    return jnp.where(offset < HALF, early, late)


def rotate(values, place, sign):
    half_dim = values.shape[-1] // 2
    freq = THETA ** (-2.0 * jnp.arange(half_dim, dtype=jnp.float32) / values.shape[-1])
    angle = place.astype(jnp.float32)[:, None] * freq[None, :]
    cosine = jnp.cos(angle)[:, None, :]
    sine = sign * jnp.sin(angle)[:, None, :]
    front = values[..., :half_dim]
    back = values[..., half_dim:]
    return jnp.concatenate([front * cosine - back * sine, back * cosine + front * sine], -1)


def norm_back(values, scale, gain, grad_out):
    weighted = grad_out * gain
    grad_in = scale * weighted - values * scale**3 * jnp.mean(weighted * values, -1, keepdims=True)
    return (grad_in, jnp.sum(grad_out * values * scale, 0))


def ring_order(count):
    return list(range(0, count, 2)) + list(reversed(range(1, count, 2)))


def ring_shift(count, step):
    order = ring_order(count)
    return [(order[i], order[(i + step) % count]) for i in range(count)]


def ring_gather(parts):
    count = lax.axis_size("ctx")
    ahead, behind = ring_shift(count, 1), ring_shift(count, -1)
    held = [list(parts)] + [[None] * len(parts) for _ in range(count - 1)]
    far = count // 2
    for p, part in enumerate(parts):
        up, down = part, part
        ups = far if p % 2 == 0 else count - 1 - far
        for step in range(1, far + 1):
            if step <= ups:
                up = lax.ppermute(up, "ctx", ahead)
                held[step][p] = up
            if step <= count - 1 - ups:
                down = lax.ppermute(down, "ctx", behind)
                held[count - step][p] = down
    return held


def add_low(left, right):
    return (left.astype(jnp.float32) + right.astype(jnp.float32)).astype(left.dtype)


def ring_sum(block, parts):
    count = lax.axis_size("ctx")
    ahead, behind = ring_shift(count, 1), ring_shift(count, -1)
    far = count // 2
    sums = []
    for p in range(parts):
        ups = far if p % 2 == 0 else count - 1 - far
        downs = count - 1 - ups
        up = block(count - ups, p)
        for step in range(ups - 1, 0, -1):
            up = lax.ppermute(up, "ctx", ahead)
            up = add_low(up, block(count - step, p))
        up = lax.ppermute(up, "ctx", ahead)
        down = block(downs, p)
        for step in range(downs - 1, 0, -1):
            down = lax.ppermute(down, "ctx", behind)
            down = add_low(down, block(step, p))
        down = lax.ppermute(down, "ctx", behind)
        own = block(0, p).astype(jnp.float32)
        sums.append(up.astype(jnp.float32) + down.astype(jnp.float32) + own)
    return sums


def spread(local):
    for axis in ("wsh", "ctx"):
        count = lax.axis_size(axis)
        me = lax.axis_index(axis)
        outer = lax.axis_size("ctx") if axis == "wsh" else 1
        bit = 1
        while bit < count:
            split = local.reshape(outer * (count // (2 * bit)), 2, -1, local.shape[-1])
            mine = (me // bit) % 2
            swap = [(i, i ^ bit) for i in range(count)]
            sent = lax.dynamic_index_in_dim(split, 1 - mine, 1, False)
            sent = lax.ppermute(sent, axis, swap)
            kept = lax.dynamic_index_in_dim(split, mine, 1, False)
            local = add_low(kept, sent).reshape(-1, local.shape[-1])
            bit *= 2
    return local.astype(jnp.float32)


PAIR = 2 * HEAD_DIM


def nt(left, right):
    return lax.dot_general(left, right, (((1,), (1,)), ((), ())), preferred_element_type=jnp.float32)


def tn(left, right):
    return lax.dot_general(left, right, (((0,), (0,)), ((), ())), preferred_element_type=jnp.float32)


def nn(left, right):
    return jnp.dot(left, right, preferred_element_type=jnp.float32)


def halves(ref, head):
    start = head * PAIR
    block = ref[0, :, start : start + PAIR]
    both = [block[:, :HEAD_DIM], block[:, HEAD_DIM:]]
    return (
        jnp.concatenate([one[:HALF] for one in both], 0),
        jnp.concatenate([one[HALF:] for one in both], 0),
    )


def key_parts(ref):
    whole = ref[...]
    count = whole.shape[0]
    early = whole[:, :HALF].reshape(count * HALF, -1)
    late = whole[:, HALF:].reshape(count * HALF, -1)
    return early, late


def weigh(scores):
    peak = jnp.max(scores[0], 0, keepdims=True)
    for more in scores[1:]:
        peak = jnp.maximum(peak, jnp.max(more, 0, keepdims=True))
    powers = [jnp.exp(part - peak) for part in scores]
    total = sum(jnp.sum(part, 0, keepdims=True) for part in powers)
    inverse = 1.0 / total
    return [part * inverse for part in powers]


def split_heads(stacked_early, stacked_late):
    return jnp.concatenate(
        [
            jnp.concatenate([stacked_early[:HALF], stacked_early[HALF:]], 1),
            jnp.concatenate([stacked_late[:HALF], stacked_late[HALF:]], 1),
        ],
        0,
    )


def fill_bias(owner, bias_early, bias_late):
    count = owner.shape[0] - 1

    @pl.when((pl.program_id(0) == 0) & (pl.program_id(1) == 0))
    def fill():
        lead = lax.broadcasted_iota(jnp.int32, (HALF, SEQ_TOK), 0) - (
            lax.broadcasted_iota(jnp.int32, (HALF, SEQ_TOK), 1) % HALF
        )
        for k in range(count):
            gap = (owner[count] - owner[k]) * HALF
            span = slice(k * HALF, (k + 1) * HALF)
            bias_early[span] = jnp.where(lead <= gap, 0.0, NEG)
            bias_late[span] = jnp.where(lead <= -gap, 0.0, NEG)


def attend_kernel(owner, query, keys, out, bias_early, bias_late):
    fill_bias(owner, bias_early, bias_late)
    early, late = key_parts(keys)
    for head in range(2):
        at = head * HEAD_DIM
        k_e, k_l = early[:, at : at + HEAD_DIM], late[:, at : at + HEAD_DIM]
        v_e, v_l = early[:, PAIR + at : PAIR + at + HEAD_DIM], late[:, PAIR + at : PAIR + at + HEAD_DIM]
        q_e, q_l = halves(query, head)
        (p_ee,) = weigh([nt(k_e, q_e) + bias_early[...]])
        p_el, p_ll = weigh([nt(k_e, q_l), nt(k_l, q_l) + bias_late[...]])
        o_e = tn(p_ee.astype(jnp.bfloat16), v_e)
        o_l = tn(p_el.astype(jnp.bfloat16), v_e) + tn(p_ll.astype(jnp.bfloat16), v_l)
        out[0, :, head * PAIR : (head + 1) * PAIR] = split_heads(o_e, o_l).astype(jnp.bfloat16)


def attend_back_kernel(
    owner, query, keys, grad, grad_query, grad_keys, bias_early, bias_late
):
    fill_bias(owner, bias_early, bias_late)
    early, late = key_parts(keys)
    scale = HEAD_DIM ** (-0.5)
    count = keys.shape[0]
    parts_e, parts_l = [], []
    for head in range(2):
        at = head * HEAD_DIM
        k_e, k_l = early[:, at : at + HEAD_DIM], late[:, at : at + HEAD_DIM]
        v_e, v_l = early[:, PAIR + at : PAIR + at + HEAD_DIM], late[:, PAIR + at : PAIR + at + HEAD_DIM]
        q_e, q_l = halves(query, head)
        d_e, d_l = halves(grad, head)
        (p_ee,) = weigh([nt(k_e, q_e) + bias_early[...]])
        p_el, p_ll = weigh([nt(k_e, q_l), nt(k_l, q_l) + bias_late[...]])
        g_ee, g_el, g_ll = nt(v_e, d_e), nt(v_e, d_l), nt(v_l, d_l)
        delta_e = jnp.sum(p_ee * g_ee, 0, keepdims=True)
        delta_l = jnp.sum(p_el * g_el, 0, keepdims=True) + jnp.sum(p_ll * g_ll, 0, keepdims=True)
        s_ee = (p_ee * (g_ee - delta_e)).astype(jnp.bfloat16)
        s_el = (p_el * (g_el - delta_l)).astype(jnp.bfloat16)
        s_ll = (p_ll * (g_ll - delta_l)).astype(jnp.bfloat16)
        gq_e = tn(s_ee, k_e) * scale
        gq_l = (tn(s_el, k_e) + tn(s_ll, k_l)) * scale
        grad_query[0, :, head * PAIR : (head + 1) * PAIR] = split_heads(gq_e, gq_l)
        gk_e = nn(s_ee, q_e) + nn(s_el, q_l)
        gk_l = nn(s_ll, q_l)
        gv_e = nn(p_ee.astype(jnp.bfloat16), d_e) + nn(p_el.astype(jnp.bfloat16), d_l)
        gv_l = nn(p_ll.astype(jnp.bfloat16), d_l)
        parts_e.append((gk_e, gv_e))
        parts_l.append((gk_l, gv_l))
    for parts, start in ((parts_e, 0), (parts_l, HALF)):
        for kind in range(2):
            joined = jnp.concatenate([parts[0][kind], parts[1][kind]], 1)
            grad_keys[:, start : start + HALF, kind * PAIR : (kind + 1) * PAIR] = (
                joined.astype(jnp.bfloat16).reshape(count, HALF, PAIR)
            )


def attend_specs(count):
    scalars = pl.BlockSpec(memory_space=pltpu.SMEM)
    rows = pl.BlockSpec((1, SEQ_TOK, 2 * PAIR), lambda s, j: (s, 0, j))
    keys = pl.BlockSpec((count, SEQ_TOK, 2 * PAIR), lambda s, j: (0, s, j))
    scratch = [pltpu.VMEM((count * HALF, SEQ_TOK), jnp.float32)] * 2
    return scalars, rows, keys, scratch


def attend(owner, query, keys):
    count = keys.shape[0]
    scalars, rows, key_rows, scratch = attend_specs(count)
    return pl.pallas_call(
        attend_kernel,
        out_shape=jax.ShapeDtypeStruct(query.shape, jnp.bfloat16),
        grid=(SEQ_GRP, KV_HEADS // 2),
        in_specs=[scalars, rows, key_rows],
        out_specs=rows,
        scratch_shapes=scratch,
        cost_estimate=pl.CostEstimate(
            flops=20 * query.size * count * SEQ_TOK,
            bytes_accessed=2 * keys.size + 4 * query.size,
            transcendentals=0,
        ),
    )(owner, query, keys)


def attend_back(owner, query, keys, grad):
    count = keys.shape[0]
    scalars, rows, key_rows, scratch = attend_specs(count)
    return pl.pallas_call(
        attend_back_kernel,
        out_shape=(
            jax.ShapeDtypeStruct(query.shape, jnp.float32),
            jax.ShapeDtypeStruct((count, SEQ_GRP * SEQ_TOK, keys.shape[2]), jnp.bfloat16),
        ),
        grid=(SEQ_GRP, KV_HEADS // 2),
        in_specs=[scalars, rows, key_rows, rows],
        out_specs=(rows, key_rows),
        scratch_shapes=scratch,
        cost_estimate=pl.CostEstimate(
            flops=30 * query.size * count * SEQ_TOK,
            bytes_accessed=4 * keys.size + 8 * query.size,
            transcendentals=0,
        ),
    )(owner, query, keys, grad)


STEP_BLOCKS = 16


def expert_kernel(
    arrived_ref,
    cot_ref,
    slot_gate_ref,
    gate_ref,
    up_ref,
    down_ref,
    produced_ref,
    back_ref,
    dots_ref,
    gate_grad_ref,
    up_grad_ref,
    down_grad_ref,
    *sums,
):
    rows = arrived_ref.shape[0] * MOST
    arrived = arrived_ref[:, 0].reshape(rows, D)
    cot = cot_ref[:, 0].reshape(rows, D)
    gate_w, up_w, down_w = gate_ref[0], up_ref[0], down_ref[0]
    gate_act = nn(arrived, gate_w)
    up_act = nn(arrived, up_w)
    sigma = jax.nn.sigmoid(gate_act)
    swish = gate_act * sigma
    hidden = (swish * up_act).astype(jnp.bfloat16)
    produced = nn(hidden, down_w).astype(jnp.bfloat16)
    produced_ref[:, 0] = produced.reshape(-1, MOST, D)
    wide = cot.astype(jnp.float32)
    dots = jnp.sum(produced.astype(jnp.float32) * wide, -1, keepdims=True)
    dots_ref[:, 0] = dots.reshape(-1, MOST, 1)
    grad_produced = (wide * slot_gate_ref[:, 0].reshape(rows, 1)).astype(jnp.bfloat16)
    grad_hidden = nt(grad_produced, down_w).astype(jnp.bfloat16).astype(jnp.float32)
    slope = sigma * (1.0 + gate_act * (1.0 - sigma))
    grad_gate = (grad_hidden * up_act * slope).astype(jnp.bfloat16)
    grad_up = (grad_hidden * swish).astype(jnp.bfloat16)
    back = nt(grad_gate, gate_w) + nt(grad_up, up_w)
    back_ref[:, 0] = back.astype(jnp.bfloat16).reshape(-1, MOST, D)
    grads = [tn(arrived, grad_gate), tn(arrived, grad_up), tn(hidden, grad_produced)]
    if sums:
        first = pl.program_id(1) == 0
        for held, grad in zip(sums, grads):
            held[...] = jnp.where(first, grad, held[...] + grad)
        grads = [held[...] for held in sums]
    quarter = gate_w.shape[1] // 4
    for k in range(4):
        span = slice(k * quarter, (k + 1) * quarter)
        gate_grad_ref[k, 0] = grads[0][:, span].astype(jnp.bfloat16)
        up_grad_ref[k, 0] = grads[1][:, span].astype(jnp.bfloat16)
        down_grad_ref[k, 0] = grads[2][span].astype(jnp.bfloat16)


def experts_pass(arrived, cot, slot_gates, gate_w, up_w, down_w):
    blocks, mine = arrived.shape[:2]
    steps = blocks // STEP_BLOCKS
    hidden = gate_w.shape[2]
    quarter = hidden // 4

    def slot_rows(width):
        return pl.BlockSpec((STEP_BLOCKS, 1, MOST, width), lambda e, c: (c, e, 0, 0))

    def per_expert(*shape):
        return pl.BlockSpec((1,) + shape, lambda e, c: (e, 0, 0))

    def pieces(*shape):
        return pl.BlockSpec((4, 1) + shape, lambda e, c: (0, e, 0, 0))

    low = jnp.bfloat16
    return pl.pallas_call(
        expert_kernel,
        grid=(mine, steps),
        in_specs=[
            slot_rows(D),
            slot_rows(D),
            slot_rows(1),
            per_expert(D, hidden),
            per_expert(D, hidden),
            per_expert(hidden, D),
        ],
        out_specs=(
            slot_rows(D),
            slot_rows(D),
            slot_rows(1),
            pieces(D, quarter),
            pieces(D, quarter),
            pieces(quarter, D),
        ),
        out_shape=(
            jax.ShapeDtypeStruct(arrived.shape, low),
            jax.ShapeDtypeStruct(arrived.shape, low),
            jax.ShapeDtypeStruct(slot_gates.shape, jnp.float32),
            jax.ShapeDtypeStruct((4, mine, D, quarter), low),
            jax.ShapeDtypeStruct((4, mine, D, quarter), low),
            jax.ShapeDtypeStruct((4, mine, quarter, D), low),
        ),
        scratch_shapes=[]
        if steps == 1
        else [
            pltpu.VMEM((D, hidden), jnp.float32),
            pltpu.VMEM((D, hidden), jnp.float32),
            pltpu.VMEM((hidden, D), jnp.float32),
        ],
        compiler_params=pltpu.CompilerParams(vmem_limit_bytes=63 * 1024 * 1024),
        cost_estimate=pl.CostEstimate(
            flops=18 * arrived.size * hidden,
            bytes_accessed=8 * arrived.size + 12 * mine * D * hidden,
            transcendentals=0,
        ),
    )(arrived, cot, slot_gates, gate_w, up_w, down_w)


def shards(
    tokens,
    routes,
    in_weight,
    out_weight,
    first_gain,
    second_gain,
    router_weight,
    gate_weight,
    up_weight,
    down_weight,
    cotangent,
):
    ctx_count = lax.axis_size("ctx")
    length = SEQ_TOK * ctx_count
    rows = SEQ_GRP * SEQ_TOK
    width_q = HEADS * HEAD_DIM
    width_k = KV_HEADS * HEAD_DIM
    my_index = lax.axis_index("ctx")
    order = ring_order(ctx_count)
    place_of = jnp.array([order.index(c) for c in range(ctx_count)], jnp.int32)
    my_place = place_of[my_index]
    table = [
        [order[(order.index(c) - k) % ctx_count] for k in range(ctx_count)] + [c]
        for c in range(ctx_count)
    ]
    owner = lax.dynamic_index_in_dim(jnp.array(table, jnp.int32), my_index, 0, False)
    local_place = dealt(my_index * SEQ_TOK + jnp.arange(SEQ_TOK, dtype=jnp.int32), length)
    upstream = cotangent.reshape(rows, D)
    chosen = jnp.any(
        routes.reshape(rows, TOP).T[:, None, :] == jnp.arange(EXPERTS, dtype=jnp.int32)[:, None], 0
    )
    gate_full, up_full, down_full = (
        lax.all_gather(gate_weight, "wsh", axis=2, tiled=True),
        lax.all_gather(up_weight, "wsh", axis=2, tiled=True),
        lax.all_gather(down_weight, "wsh", axis=1, tiled=True),
    )
    inputs = tokens.astype(jnp.float32).reshape(rows, D)
    scale_one = lax.rsqrt(jnp.mean(inputs * inputs, -1, keepdims=True) + EPS)
    normed = (inputs * scale_one * first_gain).astype(jnp.bfloat16)
    mixed = jnp.dot(normed, in_weight, preferred_element_type=jnp.float32).reshape(
        SEQ_GRP, SEQ_TOK, -1
    )
    query = rotate(
        mixed[..., :width_q].reshape(SEQ_GRP, SEQ_TOK, HEADS, HEAD_DIM), local_place, 1.0
    ).astype(jnp.bfloat16)
    query = (query * jnp.bfloat16(HEAD_DIM ** (-0.5))).reshape(SEQ_GRP, SEQ_TOK, width_q)
    key = rotate(
        mixed[..., width_q : width_q + width_k].reshape(SEQ_GRP, SEQ_TOK, KV_HEADS, HEAD_DIM),
        local_place,
        1.0,
    ).astype(jnp.bfloat16)
    value = mixed[..., width_q + width_k :].astype(jnp.bfloat16)
    pairs = (SEQ_GRP, SEQ_TOK, KV_HEADS // 2, PAIR)
    key_value = jnp.concatenate([key.reshape(pairs), value.reshape(pairs)], -1).reshape(
        rows, 2 * width_k
    )
    flags = chosen.astype(jnp.bfloat16).reshape(-1, 2 * width_k)
    flag_rows = flags.shape[0]
    flags = jnp.concatenate([flags, jnp.zeros_like(flags)], 0)
    whole = jnp.stack([held[0] for held in ring_gather([jnp.concatenate([key_value, flags], 0)])])
    whole, cot_own = lax.optimization_barrier((whole, upstream))
    cot_ring = ring_gather([cot_own])
    attended = attend(owner, query, whole)
    attended = attended.reshape(rows, width_q)
    resid = inputs + jnp.dot(attended, out_weight, preferred_element_type=jnp.float32)
    scale_two = lax.rsqrt(jnp.mean(resid * resid, -1, keepdims=True) + EPS)
    normed_two = (resid * scale_two * second_gain).astype(jnp.bfloat16)
    blocks = SEQ_GRP * ctx_count
    mine = gate_weight.shape[0]
    chosen_all = whole[:, rows : rows + flag_rows].reshape(ctx_count, EXPERTS, rows)
    chosen_my = lax.dynamic_slice_in_dim(chosen_all, my_index * mine, mine, 1)

    def by_block(values):
        split = values.reshape(ctx_count, mine, SEQ_GRP, SEQ_TOK)
        return jnp.swapaxes(split, 1, 2).reshape(blocks, mine, SEQ_TOK)

    chosen_my = by_block(chosen_my)
    before = (
        jnp.arange(SEQ_TOK, dtype=jnp.int32)[:, None] < jnp.arange(SEQ_TOK, dtype=jnp.int32)[None, :]
    ).astype(jnp.bfloat16)
    ranks = jnp.dot(
        chosen_my.reshape(blocks * mine, SEQ_TOK), before, preferred_element_type=jnp.float32
    ).reshape(blocks, mine, SEQ_TOK)
    ranks = jnp.where(chosen_my > 0, ranks, -1.0)
    normed_all = jnp.concatenate([held[0] for held in ring_gather([normed_two])])
    cot_all = jnp.concatenate([held[0] for held in cot_ring])
    logits = lax.dot_general(
        router_weight, normed_all, (((0,), (1,)), ((), ())), preferred_element_type=jnp.float32
    )
    taken = jnp.swapaxes(chosen_all, 0, 1).reshape(EXPERTS, blocks * SEQ_TOK) > 0
    picked = jnp.where(taken, logits, NEG)
    weights = jnp.where(taken, jnp.exp(picked - jnp.max(picked, 0, keepdims=True)), 0.0)
    gates_all = weights / jnp.sum(weights, 0, keepdims=True)
    gates = gates_all[:, :rows]
    gates_my = lax.dynamic_slice_in_dim(gates_all, my_index * mine, mine, 0)
    gates_my = by_block(jnp.swapaxes(gates_my.reshape(mine, ctx_count, rows), 0, 1))
    slot_ids = jnp.arange(MOST, dtype=jnp.int32).astype(jnp.float32)
    match = ranks[:, :, None, :] == slot_ids[:, None]
    chances = jnp.where(match, gates_my[:, :, None, :], 0.0)
    dispatch = match.astype(jnp.bfloat16).reshape(blocks, mine * MOST, SEQ_TOK)
    combine = chances.astype(jnp.bfloat16).reshape(blocks, mine * MOST, SEQ_TOK)
    slot_gates = jnp.sum(chances, -1, keepdims=True).astype(jnp.bfloat16).astype(jnp.float32)
    normed_blocks = normed_all.reshape(blocks, SEQ_TOK, D)
    cot_blocks = cot_all.reshape(blocks, SEQ_TOK, D)
    slot_shape = (blocks, mine, MOST, D)
    arrived, cot_slots = (
        jnp.einsum("bst,btd->bsd", dispatch, one, preferred_element_type=jnp.float32)
        .astype(jnp.bfloat16)
        .reshape(slot_shape)
        for one in (normed_blocks, cot_blocks)
    )
    produced, grad_arrived, slot_dots, gate_local, up_local, down_local = experts_pass(
        arrived, cot_slots, slot_gates, gate_full, up_full, down_full
    )
    gate_dots = jnp.sum(jnp.where(match, slot_dots, 0.0), 2)
    gate_dots = jnp.swapaxes(gate_dots.reshape(ctx_count, SEQ_GRP, mine, SEQ_TOK), 1, 2)
    ours = jnp.arange(EXPERTS, dtype=jnp.int32)[:, None] // mine == my_index
    gate_dots = jnp.where(
        ours, jnp.tile(gate_dots.reshape(ctx_count, mine, rows), (1, EXPERTS // mine, 1)), 0.0
    ).reshape(ctx_count, flag_rows, D)
    coarse = lax.reduce_precision(gate_dots, 8, 7)

    def to_tokens(matrix, slot_values):
        return jnp.einsum(
            "bst,bsd->btd",
            matrix,
            slot_values.reshape(blocks, mine * MOST, D),
            preferred_element_type=jnp.float32,
        ).astype(jnp.bfloat16).reshape(ctx_count, rows, D)

    sent_part = jnp.concatenate(
        [
            to_tokens(dispatch, grad_arrived),
            coarse.astype(jnp.bfloat16),
            (gate_dots - coarse).astype(jnp.bfloat16),
        ],
        1,
    )
    grad_sent = ring_sum(lambda k, p: sent_part[k], 1)[0]
    grad_gates = (
        grad_sent[rows : rows + flag_rows] + grad_sent[rows + flag_rows :]
    ).reshape(EXPERTS, rows)
    grad_sent = grad_sent[:rows]
    mixed_part = to_tokens(combine, produced)
    gate_grad, up_grad, down_grad = (
        lax.psum_scatter(local, "wsh", scatter_dimension=0).astype(jnp.float32)
        for local in (gate_local, up_local, down_local)
    )
    grad_logits = (gates * (grad_gates - jnp.sum(gates * grad_gates, 0, keepdims=True))).astype(
        jnp.bfloat16
    )
    router_local = lax.dot_general(
        normed_two, grad_logits, (((0,), (1,)), ((), ())), preferred_element_type=jnp.float32
    )
    grad_normed_two = grad_sent + lax.dot_general(
        grad_logits, router_weight, (((0,), (1,)), ((), ())), preferred_element_type=jnp.float32
    )
    grad_resid_norm, second_local = norm_back(resid, scale_two, second_gain, grad_normed_two)
    grad_resid = upstream.astype(jnp.float32) + grad_resid_norm
    grad_branch = grad_resid.astype(jnp.bfloat16)
    out_local = lax.dot_general(
        attended, grad_branch, (((0,), (0,)), ((), ())), preferred_element_type=jnp.float32
    )
    grad_attended = lax.dot_general(
        grad_branch, out_weight, (((1,), (1,)), ((), ())), preferred_element_type=jnp.float32
    ).astype(jnp.bfloat16)
    grad_query, grad_whole = attend_back(
        owner,
        query,
        whole,
        grad_attended.reshape(SEQ_GRP, SEQ_TOK, width_q),
    )
    grad_query = rotate(grad_query.reshape(SEQ_GRP, SEQ_TOK, HEADS, HEAD_DIM), local_place, -1.0)
    grad_query = grad_query.astype(jnp.bfloat16).reshape(rows, width_q)
    mixed_part = jnp.take(mixed_part, (my_place - place_of) % ctx_count, axis=0)
    mixed_part, grad_whole = lax.optimization_barrier((mixed_part, grad_whole))
    mixture = lax.psum_scatter(
        mixed_part.reshape(ctx_count * rows, D), "ctx", scatter_dimension=0, tiled=True
    )
    layer_out = (
        (resid + mixture.astype(jnp.float32)).astype(jnp.bfloat16).reshape(SEQ_GRP, SEQ_TOK, D)
    )
    kv_grad = ring_sum(lambda k, p: grad_whole[k], 1)[0]
    in_first = lax.dot_general(
        normed, grad_query, (((0,), (0,)), ((), ())), preferred_element_type=jnp.float32
    )
    low = jnp.bfloat16
    early = spread(
        jnp.concatenate(
            [
                in_first.astype(low),
                out_local.astype(low),
                router_local.astype(low),
                second_local[:, None].astype(low),
                jnp.zeros((D, SEQ_TOK - EXPERTS - 1), low),
            ],
            -1,
        ),
    )
    kv_grad, early = lax.optimization_barrier((kv_grad, early))
    kv_grad = kv_grad.reshape(
        SEQ_GRP, SEQ_TOK, KV_HEADS // 2, 2, PAIR
    )
    grad_key = rotate(
        kv_grad[:, :, :, 0].reshape(SEQ_GRP, SEQ_TOK, KV_HEADS, HEAD_DIM), local_place, -1.0
    )
    grad_pair = jnp.concatenate(
        [grad_key.reshape(rows, width_k), kv_grad[:, :, :, 1].reshape(rows, width_k)], -1
    ).astype(jnp.bfloat16)
    in_second = lax.dot_general(
        normed, grad_pair, (((0,), (0,)), ((), ())), preferred_element_type=jnp.float32
    )
    grad_normed = lax.dot_general(
        grad_query, in_weight[:, :width_q], (((1,), (1,)), ((), ())), preferred_element_type=jnp.float32
    ) + lax.dot_general(
        grad_pair, in_weight[:, width_q:], (((1,), (1,)), ((), ())), preferred_element_type=jnp.float32
    )
    grad_inputs_norm, first_local = norm_back(inputs, scale_one, first_gain, grad_normed)
    tokens_grad = (grad_resid + grad_inputs_norm).astype(jnp.bfloat16).reshape(SEQ_GRP, SEQ_TOK, D)
    in_second = spread(
        jnp.concatenate(
            [in_second, jnp.broadcast_to(first_local[:, None], (D, SEQ_TOK))], -1
        ).astype(jnp.bfloat16),
    )
    in_grad = jnp.concatenate([early[:, :width_q], in_second[:, : 2 * width_k]], -1)
    first_gain_grad = in_second[:, 2 * width_k]
    out_grad = early[:, width_q : width_q + D]
    small = early[:, width_q + D :]
    router_grad = small[:, :EXPERTS]
    second_gain_grad = small[:, EXPERTS]
    return (
        layer_out,
        tokens_grad,
        in_grad,
        out_grad,
        first_gain_grad,
        second_gain_grad,
        router_grad,
        gate_grad,
        up_grad,
        down_grad,
    )


def solution(mesh):
    placed = (
        P("wsh", "ctx", None),
        P("wsh", "ctx", None),
        P(),
        P(),
        P(),
        P(),
        P(),
        P("ctx", None, "wsh"),
        P("ctx", None, "wsh"),
        P("ctx", "wsh", None),
        P("wsh", "ctx", None),
    )
    return jax.shard_map(
        shards,
        mesh=mesh,
        in_specs=placed,
        out_specs=(
            P("wsh", "ctx", None),
            P("wsh", "ctx", None),
            P(("ctx", "wsh"), None),
            P(("ctx", "wsh"), None),
            P(("ctx", "wsh")),
            P(("ctx", "wsh")),
            P(("ctx", "wsh"), None),
            P("ctx", None, "wsh"),
            P("ctx", None, "wsh"),
            P("ctx", "wsh", None),
        ),
        check_vma=False,
    )
```

profile of v0, /device:TPU:0, one launch (start us, length us, event | category | flops | bytes accessed | tf_op | source)
XLA Modules:
  0.0 562.3 jit_solution(1673259063233913517)
XLA Ops:
  25.7 12.9 %collective-permute-done = bf16[272,1024]{1,0:T(8,128)(2,1)} collective-permute-done((bf16[272,1024]{1,0:T(8,128)(2,1)}, bf16[272,1024]{1,0:T(8,128)(2,1)}, u32[]{:S(2)}, u32[]{:S(2)}) %collective-permute-start) | collective-permute-done | bytes 557088 | tf_op jit(solution)/shard_map/ppermute | solution.py:69
  43.3 9.4 %collective-permute-done.1 = bf16[272,1024]{1,0:T(8,128)(2,1)} collective-permute-done((bf16[272,1024]{1,0:T(8,128)(2,1)}, bf16[272,1024]{1,0:T(8,128)(2,1)}, u32[]{:S(2)}, u32[]{:S(2)}) %collective-permute-start.1) | collective-permute-done | bytes 557088 | tf_op jit(solution)/shard_map/ppermute | solution.py:69
  57.4 8.4 %collective-permute-done.2 = bf16[272,1024]{1,0:T(8,128)(2,1)S(1)} collective-permute-done((bf16[272,1024]{1,0:T(8,128)(2,1)}, bf16[272,1024]{1,0:T(8,128)(2,1)S(1)}, u32[]{:S(2)}, u32[]{:S(2)}) %collective-permute-start.2) | collective-permute-done | bytes 557088 | tf_op jit(solution)/shard_map/ppermute | solution.py:69
  70.2 7.9 %collective-permute-done.3 = bf16[272,1024]{1,0:T(8,128)(2,1)S(1)} collective-permute-done((bf16[272,1024]{1,0:T(8,128)(2,1)S(1)}, bf16[272,1024]{1,0:T(8,128)(2,1)S(1)}, u32[]{:S(2)}, u32[]{:S(2)}) %collective-permute-start.3) | collective-permute-done | bytes 557088 | tf_op jit(solution)/shard_map/ppermute | solution.py:69
  83.4 13.4 %shard_map.204 = bf16[2,128,1024]{2,1,0:T(8,128)(2,1)} custom-call(s32[9]{0:T(128)} %fusion.69.owner, bf16[2,128,1024]{2,1,0:T(8,128)(2,1)} %copy.136.query, bf16[8,272,1024]{2,1,0:T(8,128)(2,1)} %copy-done.32), custom_call_target="tpu_custom_call" | custom-call | flops 5368709120 | bytes 5505024 | tf_op jit(solution)/shard_map/pallas_call | solution.py:255
  103.8 11.6 %collective-permute-done.7 = bf16[256,1024]{1,0:T(8,128)(2,1)S(1)} collective-permute-done((bf16[256,1024]{1,0:T(8,128)(2,1)S(1)}, bf16[256,1024]{1,0:T(8,128)(2,1)S(1)}, u32[]{:S(2)}, u32[]{:S(2)}) %collective-permute-start.7) | collective-permute-done | bytes 524320 | tf_op jit(solution)/shard_map/ppermute | solution.py:69
  119.5 7.2 %collective-permute-done.14 = bf16[256,1024]{1,0:T(8,128)(2,1)} collective-permute-done((bf16[256,1024]{1,0:T(8,128)(2,1)}, bf16[256,1024]{1,0:T(8,128)(2,1)}, u32[]{:S(2)}, u32[]{:S(2)}) %collective-permute-start.14) | collective-permute-done | bytes 524320 | tf_op jit(solution)/shard_map/ppermute | solution.py:69
  128.4 9.6 %collective-permute-done.8 = bf16[256,1024]{1,0:T(8,128)(2,1)} collective-permute-done((bf16[256,1024]{1,0:T(8,128)(2,1)S(1)}, bf16[256,1024]{1,0:T(8,128)(2,1)}, u32[]{:S(2)}, u32[]{:S(2)}) %collective-permute-start.8) | collective-permute-done | bytes 524320 | tf_op jit(solution)/shard_map/ppermute | solution.py:69
  141.1 8.0 %collective-permute-done.15 = bf16[256,1024]{1,0:T(8,128)(2,1)S(1)} collective-permute-done((bf16[256,1024]{1,0:T(8,128)(2,1)}, bf16[256,1024]{1,0:T(8,128)(2,1)S(1)}, u32[]{:S(2)}, u32[]{:S(2)}) %collective-permute-start.15) | collective-permute-done | bytes 524320 | tf_op jit(solution)/shard_map/ppermute | solution.py:69
  154.8 5.6 collective-permute-done.9
  176.2 6.7 %collective-permute-done.10 = bf16[256,1024]{1,0:T(8,128)(2,1)S(1)} collective-permute-done((bf16[256,1024]{1,0:T(8,128)(2,1)S(1)}, bf16[256,1024]{1,0:T(8,128)(2,1)S(1)}, u32[]{:S(2)}, u32[]{:S(2)}) %collective-permute-start.10) | collective-permute-done | bytes 524320 | tf_op jit(solution)/shard_map/ppermute | solution.py:69
  197.7 6.8 %convolution_convert_fusion = bf16[16,192,1024]{2,1,0:T(8,128)(2,1)} fusion(pred[16,192,128]{2,1,0:T(32,128)(4,1)S(1)} %bitcast_compare_fusion, bf16[16,128,1024]{2,1,0:T(8,128)(2,1)} %bitcast.33), kind=kOutput, calls=%fused_computation.7 | convolution fusion | flops 808452096 | bytes 10878976 | tf_op jit(solution)/shard_map/bst,btd->bsd/dot_general | solution.py:510
  204.6 4.5 convolution_convert_fusion.1
  209.1 38.1 %shard_map.205 = (bf16[16,4,48,1024]{3,2,1,0:T(8,128)(2,1)}, bf16[16,4,48,1024]{3,2,1,0:T(8,128)(2,1)}, f32[16,4,48,1]{3,2,1,0:T(8,128)}, bf16[4,4,1024,128]{3,2...) custom-call(bf16[16,4,48,1024]{3,2,1,0:T(8,128)(2,1)} %bitcast.301, ...), custom_call_target="tpu_custom_call" | custom-call | flops 28991029248 | bytes 50331648 | tf_op jit(solution)/shard_map/pallas_call | solution.py:360
  256.7 12.6 %collective-permute-done.21 = bf16[272,1024]{1,0:T(8,128)(2,1)S(1)} collective-permute-done((bf16[272,1024]{1,0:T(8,128)(2,1)S(1)}, bf16[272,1024]{1,0:T(8,128)(2,1)S(1)}, u32[]{:S(2)}, u32[]{:S(2)}) %collective-permute-start.21) | collective-permute-done | bytes 557088 | tf_op jit(solution)/shard_map/ppermute | solution.py:91
  271.3 13.5 %collective-permute-done.22 = bf16[272,1024]{1,0:T(8,128)(2,1)S(1)} collective-permute-done((bf16[272,1024]{1,0:T(8,128)(2,1)S(1)}, bf16[272,1024]{1,0:T(8,128)(2,1)S(1)}, u32[]{:S(2)}, u32[]{:S(2)}) %collective-permute-start.22) | collective-permute-done | bytes 557088 | tf_op jit(solution)/shard_map/ppermute | solution.py:91
  287.4 13.1 %collective-permute-done.23 = bf16[272,1024]{1,0:T(8,128)(2,1)S(1)} collective-permute-done((bf16[272,1024]{1,0:T(8,128)(2,1)S(1)}, bf16[272,1024]{1,0:T(8,128)(2,1)S(1)}, u32[]{:S(2)}, u32[]{:S(2)}) %collective-permute-start.23) | collective-permute-done | bytes 557088 | tf_op jit(solution)/shard_map/ppermute | solution.py:91
  304.9 7.1 %collective-permute-done.24 = bf16[272,1024]{1,0:T(8,128)(2,1)} collective-permute-done((bf16[272,1024]{1,0:T(8,128)(2,1)S(1)}, bf16[272,1024]{1,0:T(8,128)(2,1)}, u32[]{:S(2)}, u32[]{:S(2)}) %collective-permute-start.24) | collective-permute-done | bytes 557088 | tf_op jit(solution)/shard_map/ppermute | solution.py:93
  327.2 18.9 %shard_map.206 = (f32[2,128,1024]{2,1,0:T(8,128)}, bf16[8,256,1024]{2,1,0:T(8,128)(2,1)}) custom-call(s32[9]{0:T(128)} %fusion.69.owner, bf16[2,128,1024]{2,1,0:T(8,128)(2,1)} %copy.136.query, bf16[8,272,1024]{2,1,0:T(8,128)(2,1)} %copy-done.32, bf16[2,128,1024]{2,1,0:T(8,128)(2,1)} %bitcast.333), custom_call_target="tpu_custom_call" | custom-call | flops 8053063680 | bytes 11010048 | tf_op jit(solution)/shard_map/pallas_call | solution.py:273
  354.0 8.1 %concatenate.71 = bf16[16,2,32,2176]{3,2,0,1:T(8,128)(2,1)} concatenate(bf16[16,2,32,1024]{3,2,0,1:T(8,128)(2,1)} %copy.150, bf16[16,2,32,1024]{3,2,0,1:T(8,128)(2,1)} %copy.151, bf16[16,2,32,32]{3,2,0,1:T(8,128)(2,1)S(1)} %copy.152, bf16[16,2,32,1]{3,2,0,1:T(8,128)(2,1)S(1)} %copy.153, bf16[16,2,32,95]{3,2,0,1:T(8,128)(2,1)S(1)} %broadcast_in_dim.133), dimensions={3} | concatenate | bytes 8912896 | tf_op jit(solution)/shard_map/concatenate | solution.py:592
  366.9 6.1 %convolution_convert_fusion.3 = bf16[16,128,1024]{2,1,0:T(8,128)(2,1)} fusion(bf16[16,192,128]{2,1,0:T(8,128)(2,1)S(1)} %fusion.12, bf16[16,192,1024]{2,1,0:T(8,128)(2,1)} %bitcast.298), kind=kOutput, calls=%fused_computation.12 | convolution fusion | flops 807403520 | bytes 11272192 | tf_op jit(solution)/shard_map/bst,bsd->btd/dot_general | solution.py:527
  373.0 5.0 gather_fusion
  391.8 12.0 %collective-permute-done.28 = bf16[256,1024]{1,0:T(8,128)(2,1)} collective-permute-done((bf16[256,1024]{1,0:T(8,128)(2,1)S(1)}, bf16[256,1024]{1,0:T(8,128)(2,1)}, u32[]{:S(2)}, u32[]{:S(2)}) %collective-permute-start.28) | collective-permute-done | bytes 524320 | tf_op jit(solution)/shard_map/ppermute | solution.py:91
  414.7 4.8 collective-permute-done.29
  423.5 13.6 %collective-permute-done.37 = bf16[4,32,2176]{2,1,0:T(8,128)(2,1)} collective-permute-done((bf16[4,32,2176]{2,1,0:T(8,128)(2,1)}, bf16[4,32,2176]{2,1,0:T(8,128)(2,1)}, u32[]{:S(2)}, u32[]{:S(2)}) %collective-permute-start.37) | collective-permute-done | bytes 557088 | tf_op jit(solution)/shard_map/ppermute | solution.py:115
  438.5 8.6 %collective-permute-done.30 = bf16[256,1024]{1,0:T(8,128)(2,1)S(1)} collective-permute-done((bf16[256,1024]{1,0:T(8,128)(2,1)S(1)}, bf16[256,1024]{1,0:T(8,128)(2,1)S(1)}, u32[]{:S(2)}, u32[]{:S(2)}) %collective-permute-start.30) | collective-permute-done | bytes 524320 | tf_op jit(solution)/shard_map/ppermute | solution.py:91
  447.2 5.3 collective-permute-done.33
  456.2 8.7 %collective-permute-done.38 = bf16[2,32,2176]{2,1,0:T(8,128)(2,1)S(1)} collective-permute-done((bf16[2,32,2176]{2,1,0:T(8,128)(2,1)S(1)}, bf16[2,32,2176]{2,1,0:T(8,128)(2,1)S(1)}, u32[]{:S(2)}, u32[]{:S(2)}) %collective-permute-start.38) | collective-permute-done | bytes 278560 | tf_op jit(solution)/shard_map/ppermute | solution.py:115
  465.1 14.7 %collective-permute-done.31 = bf16[256,1024]{1,0:T(8,128)(2,1)S(1)} collective-permute-done((bf16[256,1024]{1,0:T(8,128)(2,1)S(1)}, bf16[256,1024]{1,0:T(8,128)(2,1)S(1)}, u32[]{:S(2)}, u32[]{:S(2)}) %collective-permute-start.31) | collective-permute-done | bytes 524320 | tf_op jit(solution)/shard_map/ppermute | solution.py:93
  479.8 7.9 %collective-permute-done.34 = bf16[256,1024]{1,0:T(8,128)(2,1)S(1)} collective-permute-done((bf16[256,1024]{1,0:T(8,128)(2,1)S(1)}, bf16[256,1024]{1,0:T(8,128)(2,1)S(1)}, u32[]{:S(2)}, u32[]{:S(2)}) %collective-permute-start.34) | collective-permute-done | bytes 524320 | tf_op jit(solution)/shard_map/ppermute | solution.py:98
  521.8 10.7 %collective-permute-done.41 = bf16[8,32,1152]{2,1,0:T(8,128)(2,1)S(1)} collective-permute-done((bf16[8,32,1152]{2,1,0:T(8,128)(2,1)S(1)}, bf16[8,32,1152]{2,1,0:T(8,128)(2,1)S(1)}, u32[]{:S(2)}, u32[]{:S(2)}) %collective-permute-start.41) | collective-permute-done | bytes 589856 | tf_op jit(solution)/shard_map/ppermute | solution.py:115
  535.9 5.1 collective-permute-done.42
  (357 shorter events, 220.8 us)
Async XLA Ops:
  7.2 201.9 %all-gather.4.cloned.1.call-start = ((), (), s32[]{:S(2)}) async-start(), calls=%async_computation.4 | async-start | bytes 5242880 | tf_op jit(solution)/shard_map/all_gather | solution.py:436
  7.9 201.2 %all-gather.6.cloned.1.call-start = ((), (), s32[]{:S(2)}) async-start(), calls=%async_computation.5 | async-start | bytes 5242880 | tf_op jit(solution)/shard_map/all_gather | solution.py:437
  8.7 200.4 %all-gather.8.cloned.1.call-start = ((), (), s32[]{:S(2)}) async-start(), calls=%async_computation.6 | async-start | bytes 5242880 | tf_op jit(solution)/shard_map/all_gather | solution.py:438
  22.7 15.9 %collective-permute-start = (bf16[272,1024]{1,0:T(8,128)(2,1)}, bf16[272,1024]{1,0:T(8,128)(2,1)}, u32[]{:S(2)}, u32[]{:S(2)}) collective-permute-start(bf16[272,1024]{1,0:T(8,128)(2,1)} %maximum_maximum_fusion), channel_id=1, source_target_pairs={{0,8},{8,16},{16,24},{24,28},{28,20},{20,12},{12,4},{4,0},{1,9},{9... | collective-permute-start | bytes 1671176 | tf_op jit(solution)/shard_map/ppermute | solution.py:69
  40.7 492.4 %reduce-scatter.11.cloned.1.call-start = ((), (), s32[]{:S(2)}) async-start(), calls=%async_computation.10 | async-start | bytes 5242880 | tf_op jit(solution)/shard_map/reduce_scatter | solution.py:549
  102.2 24.6 %collective-permute-start.14 = (bf16[256,1024]{1,0:T(8,128)(2,1)}, bf16[256,1024]{1,0:T(8,128)(2,1)}, u32[]{:S(2)}, u32[]{:S(2)}) collective-permute-start(bf16[256,1024]{1,0:T(8,128)(2,1)} %bitcast.18), channel_id=1, source_target_pairs={{0,8},{8,16},{16,24},{24,28},{28,20},{20,12},{12,4},{4,0},{1,9},{9... | collective-permute-start | bytes 1572872 | tf_op jit(solution)/shard_map/ppermute | solution.py:69
  115.4 22.6 %collective-permute-start.8 = (bf16[256,1024]{1,0:T(8,128)(2,1)S(1)}, bf16[256,1024]{1,0:T(8,128)(2,1)}, u32[]{:S(2)}, u32[]{:S(2)}) collective-permute-start(bf16[256,1024]{1,0:T(8,128)(2,1)S(1)} %collective-permute-done.7), channel_id=1, source_target_pairs={{0,8},{8,16},{16,24},{24,28},{28,20},{20,12},{12,4},{4,0},{1,9},{9... | collective-permute-start | bytes 1572872 | tf_op jit(solution)/shard_map/ppermute | solution.py:69
  117.0 22.6 %collective-permute-start.11 = (bf16[256,1024]{1,0:T(8,128)(2,1)S(1)}, bf16[256,1024]{1,0:T(8,128)(2,1)S(1)}, u32[]{:S(2)}, u32[]{:S(2)}) collective-permute-start(bf16[256,1024]{1,0:T(8,128)(2,1)S(1)} %get-tuple-element.45), channel_id=1, source_target_pairs={{0,4},{8,0},{16,8},{24,16},{28,24},{20,28},{12,20},{4,12},{1,5},{9... | collective-permute-start | bytes 1572872 | tf_op jit(solution)/shard_map/ppermute | solution.py:72
  117.5 22.7 %collective-permute-start.18 = (bf16[256,1024]{1,0:T(8,128)(2,1)}, bf16[256,1024]{1,0:T(8,128)(2,1)S(1)}, u32[]{:S(2)}, u32[]{:S(2)}) collective-permute-start(bf16[256,1024]{1,0:T(8,128)(2,1)} %bitcast.18), channel_id=1, source_target_pairs={{0,4},{8,0},{16,8},{24,16},{28,24},{20,28},{12,20},{4,12},{1,5},{9... | collective-permute-start | bytes 1572872 | tf_op jit(solution)/shard_map/ppermute | solution.py:72
  126.8 22.4 %collective-permute-start.15 = (bf16[256,1024]{1,0:T(8,128)(2,1)}, bf16[256,1024]{1,0:T(8,128)(2,1)S(1)}, u32[]{:S(2)}, u32[]{:S(2)}) collective-permute-start(bf16[256,1024]{1,0:T(8,128)(2,1)} %collective-permute-done.14), channel_id=1, source_target_pairs={{0,8},{8,16},{16,24},{24,28},{28,20},{20,12},{12,4},{4,0},{1,9},{9... | collective-permute-start | bytes 1572872 | tf_op jit(solution)/shard_map/ppermute | solution.py:69
  138.0 22.4 %collective-permute-start.9 = (bf16[256,1024]{1,0:T(8,128)(2,1)}, bf16[256,1024]{1,0:T(8,128)(2,1)S(1)}, u32[]{:S(2)}, u32[]{:S(2)}) collective-permute-start(bf16[256,1024]{1,0:T(8,128)(2,1)} %collective-permute-done.8), channel_id=1, source_target_pairs={{0,8},{8,16},{16,24},{24,28},{28,20},{20,12},{12,4},{4,0},{1,9},{9... | collective-permute-start | bytes 1572872 | tf_op jit(solution)/shard_map/ppermute | solution.py:69
  139.6 24.2 %collective-permute-start.12 = (bf16[256,1024]{1,0:T(8,128)(2,1)S(1)}, bf16[256,1024]{1,0:T(8,128)(2,1)S(1)}, u32[]{:S(2)}, u32[]{:S(2)}) collective-permute-start(bf16[256,1024]{1,0:T(8,128)(2,1)S(1)} %collective-permute-done.11), channel_id=1, source_target_pairs={{0,4},{8,0},{16,8},{24,16},{28,24},{20,28},{12,20},{4,12},{1,5},{9... | collective-permute-start | bytes 1572872 | tf_op jit(solution)/shard_map/ppermute | solution.py:72
  140.1 26.0 %collective-permute-start.19 = (bf16[256,1024]{1,0:T(8,128)(2,1)S(1)}, bf16[256,1024]{1,0:T(8,128)(2,1)S(1)}, u32[]{:S(2)}, u32[]{:S(2)}) collective-permute-start(bf16[256,1024]{1,0:T(8,128)(2,1)S(1)} %collective-permute-done.18), channel_id=1, source_target_pairs={{0,4},{8,0},{16,8},{24,16},{28,24},{20,28},{12,20},{4,12},{1,5},{9... | collective-permute-start | bytes 1572872 | tf_op jit(solution)/shard_map/ppermute | solution.py:72
  149.1 22.6 %collective-permute-start.16 = (bf16[256,1024]{1,0:T(8,128)(2,1)S(1)}, bf16[256,1024]{1,0:T(8,128)(2,1)}, u32[]{:S(2)}, u32[]{:S(2)}) collective-permute-start(bf16[256,1024]{1,0:T(8,128)(2,1)S(1)} %collective-permute-done.15), channel_id=1, source_target_pairs={{0,8},{8,16},{16,24},{24,28},{28,20},{20,12},{12,4},{4,0},{1,9},{9... | collective-permute-start | bytes 1572872 | tf_op jit(solution)/shard_map/ppermute | solution.py:69
  160.4 22.5 %collective-permute-start.10 = (bf16[256,1024]{1,0:T(8,128)(2,1)S(1)}, bf16[256,1024]{1,0:T(8,128)(2,1)S(1)}, u32[]{:S(2)}, u32[]{:S(2)}) collective-permute-start(bf16[256,1024]{1,0:T(8,128)(2,1)S(1)} %collective-permute-done.9), channel_id=1, source_target_pairs={{0,8},{8,16},{16,24},{24,28},{28,20},{20,12},{12,4},{4,0},{1,9},{9... | collective-permute-start | bytes 1572872 | tf_op jit(solution)/shard_map/ppermute | solution.py:69
  163.8 19.9 %collective-permute-start.13 = (bf16[256,1024]{1,0:T(8,128)(2,1)S(1)}, bf16[256,1024]{1,0:T(8,128)(2,1)S(1)}, u32[]{:S(2)}, u32[]{:S(2)}) collective-permute-start(bf16[256,1024]{1,0:T(8,128)(2,1)S(1)} %collective-permute-done.12), channel_id=1, source_target_pairs={{0,4},{8,0},{16,8},{24,16},{28,24},{20,28},{12,20},{4,12},{1,5},{9... | collective-permute-start | bytes 1572872 | tf_op jit(solution)/shard_map/ppermute | solution.py:72
  166.2 28.0 %collective-permute-start.20 = (bf16[256,1024]{1,0:T(8,128)(2,1)S(1)}, bf16[256,1024]{1,0:T(8,128)(2,1)}, u32[]{:S(2)}, u32[]{:S(2)}) collective-permute-start(bf16[256,1024]{1,0:T(8,128)(2,1)S(1)} %collective-permute-done.19), channel_id=1, source_target_pairs={{0,4},{8,0},{16,8},{24,16},{28,24},{20,28},{12,20},{4,12},{1,5},{9... | collective-permute-start | bytes 1572872 | tf_op jit(solution)/shard_map/ppermute | solution.py:72
  171.7 20.6 %collective-permute-start.17 = (bf16[256,1024]{1,0:T(8,128)(2,1)}, bf16[256,1024]{1,0:T(8,128)(2,1)}, u32[]{:S(2)}, u32[]{:S(2)}) collective-permute-start(bf16[256,1024]{1,0:T(8,128)(2,1)} %collective-permute-done.16), channel_id=1, source_target_pairs={{0,8},{8,16},{16,24},{24,28},{28,20},{20,12},{12,4},{4,0},{1,9},{9... | collective-permute-start | bytes 1572872 | tf_op jit(solution)/shard_map/ppermute | solution.py:69
  247.3 293.9 %reduce-scatter.9.cloned.1.call-start = ((), (), s32[]{:S(2)}) async-start(), calls=%async_computation.9 | async-start | bytes 5242880 | tf_op jit(solution)/shard_map/reduce_scatter | solution.py:549
  247.9 298.6 %reduce-scatter.7.cloned.1.call-start = ((), (), s32[]{:S(2)}) async-start(), calls=%async_computation.8 | async-start | bytes 5242880 | tf_op jit(solution)/shard_map/reduce_scatter | solution.py:549
  269.6 15.2 %collective-permute-start.22 = (bf16[272,1024]{1,0:T(8,128)(2,1)S(1)}, bf16[272,1024]{1,0:T(8,128)(2,1)S(1)}, u32[]{:S(2)}, u32[]{:S(2)}) collective-permute-start(bf16[272,1024]{1,0:T(8,128)(2,1)S(1)} %fusion.26), channel_id=1, source_target_pairs={{0,8},{8,16},{16,24},{24,28},{28,20},{20,12},{12,4},{4,0},{1,9},{9... | collective-permute-start | bytes 1671176 | tf_op jit(solution)/shard_map/ppermute | solution.py:91
  304.4 248.9 %reduce-scatter.5.cloned.1.call-start = ((), (), s32[]{:S(2)}) async-start(), calls=%async_computation.7 | async-start | bytes 4718592 | tf_op jit(solution)/shard_map/reduce_scatter | solution.py:580
  383.4 27.5 %collective-permute-start.36 = (bf16[8,32,2176]{2,1,0:T(8,128)(2,1)}, bf16[8,32,2176]{2,1,0:T(8,128)(2,1)}, u32[]{:S(2)}, u32[]{:S(2)}) collective-permute-start(bf16[8,32,2176]{2,1,0:T(8,128)(2,1)} %dynamic-slice_bitcast_fusion.1), channel_id=1, source_target_pairs={{0,2},{1,3},{2,0},{3,1},{4,6},{5,7},{6,4},{7,5},{8,10},{9,11},{10,... | collective-permute-start | bytes 3342344 | tf_op jit(solution)/shard_map/ppermute | solution.py:115
  391.2 23.5 %collective-permute-start.32 = (bf16[256,1024]{1,0:T(8,128)(2,1)}, bf16[256,1024]{1,0:T(8,128)(2,1)}, u32[]{:S(2)}, u32[]{:S(2)}) collective-permute-start(bf16[256,1024]{1,0:T(8,128)(2,1)} %get-tuple-element.57), channel_id=1, source_target_pairs={{0,4},{8,0},{16,8},{24,16},{28,24},{20,28},{12,20},{4,12},{1,5},{9... | collective-permute-start | bytes 1572872 | tf_op jit(solution)/shard_map/ppermute | solution.py:96
  414.6 22.4 %collective-permute-start.37 = (bf16[4,32,2176]{2,1,0:T(8,128)(2,1)}, bf16[4,32,2176]{2,1,0:T(8,128)(2,1)}, u32[]{:S(2)}, u32[]{:S(2)}) collective-permute-start(bf16[4,32,2176]{2,1,0:T(8,128)(2,1)} %dynamic-slice_bitcast_fusion.3), channel_id=1, source_target_pairs={{0,4},{4,0},{8,12},{12,8},{16,20},{20,16},{24,28},{28,24},{1,5},{5... | collective-permute-start | bytes 1671176 | tf_op jit(solution)/shard_map/ppermute | solution.py:115
  421.4 25.8 %collective-permute-start.30 = (bf16[256,1024]{1,0:T(8,128)(2,1)S(1)}, bf16[256,1024]{1,0:T(8,128)(2,1)S(1)}, u32[]{:S(2)}, u32[]{:S(2)}) collective-permute-start(bf16[256,1024]{1,0:T(8,128)(2,1)S(1)} %get-tuple-element.54), channel_id=1, source_target_pairs={{0,8},{8,16},{16,24},{24,28},{28,20},{20,12},{12,4},{4,0},{1,9},{9... | collective-permute-start | bytes 1572872 | tf_op jit(solution)/shard_map/ppermute | solution.py:91
  421.9 30.6 %collective-permute-start.33 = (bf16[256,1024]{1,0:T(8,128)(2,1)S(1)}, bf16[256,1024]{1,0:T(8,128)(2,1)S(1)}, u32[]{:S(2)}, u32[]{:S(2)}) collective-permute-start(bf16[256,1024]{1,0:T(8,128)(2,1)S(1)} %get-tuple-element.55), channel_id=1, source_target_pairs={{0,4},{8,0},{16,8},{24,16},{28,24},{20,28},{12,20},{4,12},{1,5},{9... | collective-permute-start | bytes 1572872 | tf_op jit(solution)/shard_map/ppermute | solution.py:96
  438.4 26.5 %collective-permute-start.38 = (bf16[2,32,2176]{2,1,0:T(8,128)(2,1)S(1)}, bf16[2,32,2176]{2,1,0:T(8,128)(2,1)S(1)}, u32[]{:S(2)}, u32[]{:S(2)}) collective-permute-start(bf16[2,32,2176]{2,1,0:T(8,128)(2,1)S(1)} %dynamic-slice_bitcast_fusion.5), channel_id=1, source_target_pairs={{0,8},{4,12},{8,0},{12,4},{16,24},{20,28},{24,16},{28,20},{1,9},{5... | collective-permute-start | bytes 835592 | tf_op jit(solution)/shard_map/ppermute | solution.py:115
  454.1 25.6 %collective-permute-start.31 = (bf16[256,1024]{1,0:T(8,128)(2,1)S(1)}, bf16[256,1024]{1,0:T(8,128)(2,1)S(1)}, u32[]{:S(2)}, u32[]{:S(2)}) collective-permute-start(bf16[256,1024]{1,0:T(8,128)(2,1)S(1)} %get-tuple-element.52), channel_id=1, source_target_pairs={{0,8},{8,16},{16,24},{24,28},{28,20},{20,12},{12,4},{4,0},{1,9},{9... | collective-permute-start | bytes 1572872 | tf_op jit(solution)/shard_map/ppermute | solution.py:93
  454.2 33.5 %collective-permute-start.34 = (bf16[256,1024]{1,0:T(8,128)(2,1)S(1)}, bf16[256,1024]{1,0:T(8,128)(2,1)S(1)}, u32[]{:S(2)}, u32[]{:S(2)}) collective-permute-start(bf16[256,1024]{1,0:T(8,128)(2,1)S(1)} %get-tuple-element.53), channel_id=1, source_target_pairs={{0,4},{8,0},{16,8},{24,16},{28,24},{20,28},{12,20},{4,12},{1,5},{9... | collective-permute-start | bytes 1572872 | tf_op jit(solution)/shard_map/ppermute | solution.py:98
  465.0 24.9 %collective-permute-start.39 = (bf16[1,32,2176]{2,1,0:T(8,128)(2,1)S(1)}, bf16[1,32,2176]{2,1,0:T(8,128)(2,1)S(1)}, u32[]{:S(2)}, u32[]{:S(2)}) collective-permute-start(bf16[1,32,2176]{2,1,0:T(8,128)(2,1)S(1)} %constant_dynamic-slice_fusion.2), channel_id=1, source_target_pairs={{0,16},{4,20},{8,24},{12,28},{16,0},{20,4},{24,8},{28,12},{1,17},{... | collective-permute-start | bytes 417800 | tf_op jit(solution)/shard_map/ppermute | solution.py:115
  517.1 15.4 %collective-permute-start.41 = (bf16[8,32,1152]{2,1,0:T(8,128)(2,1)S(1)}, bf16[8,32,1152]{2,1,0:T(8,128)(2,1)S(1)}, u32[]{:S(2)}, u32[]{:S(2)}) collective-permute-start(bf16[8,32,1152]{2,1,0:T(8,128)(2,1)S(1)} %dynamic-slice_bitcast_fusion.2), channel_id=1, source_target_pairs={{0,2},{1,3},{2,0},{3,1},{4,6},{5,7},{6,4},{7,5},{8,10},{9,11},{10,... | collective-permute-start | bytes 1769480 | tf_op jit(solution)/shard_map/ppermute | solution.py:115
  (69 other events, 1052.9 us)
Sparse Core Ops, SparseCore 0:
  9.6 37.7 all-gather.3
  48.9 34.9 all-gather.5
  85.5 34.4 all-gather.7
  247.4 44.7 reduce-scatter.10
  294.6 44.5 reduce-scatter.8
  341.6 44.5 reduce-scatter.6
  414.8 114.8 reduce-scatter.4
where the time goes:
time: 571 us; the launch traced here: 562 us
  waiting for transfers between devices  248 us (43%)
  local copies, waits for them, and re-layouts  90.5 us (16%)
  Pallas kernels  70.4 us (12%)
  other arithmetic  47.8 us (8%)
  starting transfers between devices  46.5 us (8%)
  matrix products  43.6 us (8%)
  between operations  15.5 us (3%)
    ppermute x12, waiting for transfers between devices, ring_gather(): up = lax.ppermute(up, 'ctx', ahead)  91.2 us
    ppermute x8, waiting for transfers between devices, ring_sum(): up = lax.ppermute(up, 'ctx', ahead)  86.4 us
    ppermute x10, waiting for transfers between devices, spread(): sent = lax.ppermute(sent, axis, swap)  50.2 us
    pallas_call x1, Pallas kernels, experts_pass(): pl.pallas_call(expert_kernel, grid=(mine, steps), in_specs=[slot_rows(D),...  38.1 us
    unnamed x121, local copies, waits for them, and re-layouts  32.8 us
    ppermute x12, starting transfers between devices, ring_gather(): up = lax.ppermute(up, 'ctx', ahead)  20.3 us
    pallas_call x1, Pallas kernels, attend_back(): pl.pallas_call(attend_back_kernel, out_shape=(jax.ShapeDtypeStruct(query....  18.9 us
    ppermute x6, waiting for transfers between devices, ring_sum(): down = lax.ppermute(down, 'ctx', behind)  16.1 us
  transfers between devices with their start and end apart: 52, of which 33 were waited for; matrix products, arithmetic and copies ran while one was open for 31% of the time, Pallas kernels for 6%

commit v1 on v0

--- a/solution.py
+++ b/solution.py
@@ -575,14 +575,6 @@
     )
     grad_query = rotate(grad_query.reshape(SEQ_GRP, SEQ_TOK, HEADS, HEAD_DIM), local_place, -1.0)
     grad_query = grad_query.astype(jnp.bfloat16).reshape(rows, width_q)
-    mixed_part = jnp.take(mixed_part, (my_place - place_of) % ctx_count, axis=0)
-    mixed_part, grad_whole = lax.optimization_barrier((mixed_part, grad_whole))
-    mixture = lax.psum_scatter(
-        mixed_part.reshape(ctx_count * rows, D), "ctx", scatter_dimension=0, tiled=True
-    )
-    layer_out = (
-        (resid + mixture.astype(jnp.float32)).astype(jnp.bfloat16).reshape(SEQ_GRP, SEQ_TOK, D)
-    )
     kv_grad = ring_sum(lambda k, p: grad_whole[k], 1)[0]
     in_first = lax.dot_general(
         normed, grad_query, (((0,), (0,)), ((), ())), preferred_element_type=jnp.float32
@@ -600,7 +592,14 @@
             -1,
         ),
     )
-    kv_grad, early = lax.optimization_barrier((kv_grad, early))
+    mixed_part = jnp.take(mixed_part, (my_place - place_of) % ctx_count, axis=0, mode="clip")
+    kv_grad, early, mixed_part = lax.optimization_barrier((kv_grad, early, mixed_part))
+    mixture = lax.psum_scatter(
+        mixed_part.reshape(ctx_count * rows, D), "ctx", scatter_dimension=0, tiled=True
+    )
+    layer_out = (
+        (resid + mixture.astype(jnp.float32)).astype(jnp.bfloat16).reshape(SEQ_GRP, SEQ_TOK, D)
+    )
     kv_grad = kv_grad.reshape(
         SEQ_GRP, SEQ_TOK, KV_HEADS // 2, 2, PAIR
     )

time: 571 us -> 587 us (1.028)
  waiting for transfers between devices: 248 us -> 257 us
    reduce_scatter x1, waiting for transfers between devices: 0.01 us -> 33.4 us  [shards(): lax.psum_scatter(mixed_part.reshape(ctx_count * rows, D), 'ctx', scatter_...]
    ppermute x8, waiting for transfers between devices: 86.4 us -> 57.8 us  [ring_sum(): up = lax.ppermute(up, 'ctx', ahead)]
  transfers between devices with their start and end apart: 52 -> 52, of which waited for: 33 -> 32; matrix products, arithmetic and copies ran while one was open for 31% -> 30% of each run, Pallas kernels for 6% -> 6%
where the time goes in v1:
time: 587 us; the launch traced here: 579 us
  waiting for transfers between devices  257 us (44%)
  local copies, waits for them, and re-layouts  91 us (16%)
  Pallas kernels  70.3 us (12%)
  starting transfers between devices  52.3 us (9%)
  other arithmetic  51.9 us (9%)
  matrix products  40.3 us (7%)
  between operations  15.5 us (3%)
    ppermute x12, waiting for transfers between devices, ring_gather(): up = lax.ppermute(up, 'ctx', ahead)  91.1 us
    ppermute x8, waiting for transfers between devices, ring_sum(): up = lax.ppermute(up, 'ctx', ahead)  57.8 us
    ppermute x10, waiting for transfers between devices, spread(): sent = lax.ppermute(sent, axis, swap)  53.5 us
    pallas_call x1, Pallas kernels, experts_pass(): pl.pallas_call(expert_kernel, grid=(mine, steps), in_specs=[slot_rows(D),...  38.1 us
    unnamed x121, local copies, waits for them, and re-layouts  33.5 us
    reduce_scatter x1, waiting for transfers between devices, shards(): lax.psum_scatter(mixed_part.reshape(ctx_count * rows, D), 'ctx', scatter_...  33.4 us
    ppermute x12, starting transfers between devices, ring_gather(): up = lax.ppermute(up, 'ctx', ahead)  20.7 us
    pallas_call x1, Pallas kernels, attend_back(): pl.pallas_call(attend_back_kernel, out_shape=(jax.ShapeDtypeStruct(query....  18.9 us
  transfers between devices with their start and end apart: 52, of which 32 were waited for; matrix products, arithmetic and copies ran while one was open for 30% of the time, Pallas kernels for 6%

profile of v1, /device:TPU:0, one launch (start us, length us, event | category | flops | bytes accessed | tf_op | source)
XLA Modules:
  0.0 578.6 jit_solution(6574512580661466518)
XLA Ops:
  25.8 12.9 %collective-permute-done = bf16[272,1024]{1,0:T(8,128)(2,1)} collective-permute-done((bf16[272,1024]{1,0:T(8,128)(2,1)}, bf16[272,1024]{1,0:T(8,128)(2,1)}, u32[]{:S(2)}, u32[]{:S(2)}) %collective-permute-start) | collective-permute-done | bytes 557088 | tf_op jit(solution)/shard_map/ppermute | solution.py:69
  43.3 9.4 %collective-permute-done.1 = bf16[272,1024]{1,0:T(8,128)(2,1)} collective-permute-done((bf16[272,1024]{1,0:T(8,128)(2,1)}, bf16[272,1024]{1,0:T(8,128)(2,1)}, u32[]{:S(2)}, u32[]{:S(2)}) %collective-permute-start.1) | collective-permute-done | bytes 557088 | tf_op jit(solution)/shard_map/ppermute | solution.py:69
  57.5 8.4 %collective-permute-done.2 = bf16[272,1024]{1,0:T(8,128)(2,1)S(1)} collective-permute-done((bf16[272,1024]{1,0:T(8,128)(2,1)}, bf16[272,1024]{1,0:T(8,128)(2,1)S(1)}, u32[]{:S(2)}, u32[]{:S(2)}) %collective-permute-start.2) | collective-permute-done | bytes 557088 | tf_op jit(solution)/shard_map/ppermute | solution.py:69
  70.2 7.9 %collective-permute-done.3 = bf16[272,1024]{1,0:T(8,128)(2,1)S(1)} collective-permute-done((bf16[272,1024]{1,0:T(8,128)(2,1)S(1)}, bf16[272,1024]{1,0:T(8,128)(2,1)S(1)}, u32[]{:S(2)}, u32[]{:S(2)}) %collective-permute-start.3) | collective-permute-done | bytes 557088 | tf_op jit(solution)/shard_map/ppermute | solution.py:69
  83.5 13.4 %shard_map.204 = bf16[2,128,1024]{2,1,0:T(8,128)(2,1)} custom-call(s32[9]{0:T(128)} %fusion.69.owner, bf16[2,128,1024]{2,1,0:T(8,128)(2,1)} %copy.136.query, bf16[8,272,1024]{2,1,0:T(8,128)(2,1)} %copy-done.32), custom_call_target="tpu_custom_call" | custom-call | flops 5368709120 | bytes 5505024 | tf_op jit(solution)/shard_map/pallas_call | solution.py:255
  103.9 11.6 %collective-permute-done.7 = bf16[256,1024]{1,0:T(8,128)(2,1)S(1)} collective-permute-done((bf16[256,1024]{1,0:T(8,128)(2,1)S(1)}, bf16[256,1024]{1,0:T(8,128)(2,1)S(1)}, u32[]{:S(2)}, u32[]{:S(2)}) %collective-permute-start.7) | collective-permute-done | bytes 524320 | tf_op jit(solution)/shard_map/ppermute | solution.py:69
  119.6 7.2 %collective-permute-done.14 = bf16[256,1024]{1,0:T(8,128)(2,1)} collective-permute-done((bf16[256,1024]{1,0:T(8,128)(2,1)}, bf16[256,1024]{1,0:T(8,128)(2,1)}, u32[]{:S(2)}, u32[]{:S(2)}) %collective-permute-start.14) | collective-permute-done | bytes 524320 | tf_op jit(solution)/shard_map/ppermute | solution.py:69
  128.5 9.6 %collective-permute-done.8 = bf16[256,1024]{1,0:T(8,128)(2,1)} collective-permute-done((bf16[256,1024]{1,0:T(8,128)(2,1)S(1)}, bf16[256,1024]{1,0:T(8,128)(2,1)}, u32[]{:S(2)}, u32[]{:S(2)}) %collective-permute-start.8) | collective-permute-done | bytes 524320 | tf_op jit(solution)/shard_map/ppermute | solution.py:69
  141.2 8.0 %collective-permute-done.15 = bf16[256,1024]{1,0:T(8,128)(2,1)S(1)} collective-permute-done((bf16[256,1024]{1,0:T(8,128)(2,1)}, bf16[256,1024]{1,0:T(8,128)(2,1)S(1)}, u32[]{:S(2)}, u32[]{:S(2)}) %collective-permute-start.15) | collective-permute-done | bytes 524320 | tf_op jit(solution)/shard_map/ppermute | solution.py:69
  154.9 5.5 collective-permute-done.9
  167.9 3.9 collective-permute-done.16
  176.2 6.7 %collective-permute-done.10 = bf16[256,1024]{1,0:T(8,128)(2,1)S(1)} collective-permute-done((bf16[256,1024]{1,0:T(8,128)(2,1)S(1)}, bf16[256,1024]{1,0:T(8,128)(2,1)S(1)}, u32[]{:S(2)}, u32[]{:S(2)}) %collective-permute-start.10) | collective-permute-done | bytes 524320 | tf_op jit(solution)/shard_map/ppermute | solution.py:69
  198.0 4.5 convolution_convert_fusion.1
  202.5 6.6 %convolution_convert_fusion = bf16[16,192,1024]{2,1,0:T(8,128)(2,1)} fusion(pred[16,192,128]{2,1,0:T(32,128)(4,1)S(1)} %bitcast_compare_fusion, bf16[16,128,1024]{2,1,0:T(8,128)(2,1)} %bitcast.25), kind=kOutput, calls=%fused_computation.6 | convolution fusion | flops 808452096 | bytes 10878976 | tf_op jit(solution)/shard_map/bst,btd->bsd/dot_general | solution.py:510
  209.0 38.1 %shard_map.205 = (bf16[16,4,48,1024]{3,2,1,0:T(8,128)(2,1)}, bf16[16,4,48,1024]{3,2,1,0:T(8,128)(2,1)}, f32[16,4,48,1]{3,2,1,0:T(8,128)}, bf16[4,4,1024,128]{3,2...) custom-call(bf16[16,4,48,1024]{3,2,1,0:T(8,128)(2,1)} %bitcast.300, ...), custom_call_target="tpu_custom_call" | custom-call | flops 28991029248 | bytes 50331648 | tf_op jit(solution)/shard_map/pallas_call | solution.py:360
  249.9 4.1 convolution_convert_fusion.3
  260.2 11.9 %collective-permute-done.21 = bf16[272,1024]{1,0:T(8,128)(2,1)} collective-permute-done((bf16[272,1024]{1,0:T(8,128)(2,1)S(1)}, bf16[272,1024]{1,0:T(8,128)(2,1)}, u32[]{:S(2)}, u32[]{:S(2)}) %collective-permute-start.21) | collective-permute-done | bytes 557088 | tf_op jit(solution)/shard_map/ppermute | solution.py:91
  275.1 13.2 %collective-permute-done.22 = bf16[272,1024]{1,0:T(8,128)(2,1)S(1)} collective-permute-done((bf16[272,1024]{1,0:T(8,128)(2,1)S(1)}, bf16[272,1024]{1,0:T(8,128)(2,1)S(1)}, u32[]{:S(2)}, u32[]{:S(2)}) %collective-permute-start.22) | collective-permute-done | bytes 557088 | tf_op jit(solution)/shard_map/ppermute | solution.py:91
  292.0 12.8 %collective-permute-done.23 = bf16[272,1024]{1,0:T(8,128)(2,1)S(1)} collective-permute-done((bf16[272,1024]{1,0:T(8,128)(2,1)S(1)}, bf16[272,1024]{1,0:T(8,128)(2,1)S(1)}, u32[]{:S(2)}, u32[]{:S(2)}) %collective-permute-start.23) | collective-permute-done | bytes 557088 | tf_op jit(solution)/shard_map/ppermute | solution.py:91
  309.8 7.2 %collective-permute-done.27 = bf16[272,1024]{1,0:T(8,128)(2,1)} collective-permute-done((bf16[272,1024]{1,0:T(8,128)(2,1)S(1)}, bf16[272,1024]{1,0:T(8,128)(2,1)}, u32[]{:S(2)}, u32[]{:S(2)}) %collective-permute-start.27) | collective-permute-done | bytes 557088 | tf_op jit(solution)/shard_map/ppermute | solution.py:98
  325.3 18.9 %shard_map.206 = (f32[2,128,1024]{2,1,0:T(8,128)}, bf16[8,256,1024]{2,1,0:T(8,128)(2,1)}) custom-call(s32[9]{0:T(128)} %fusion.69.owner, bf16[2,128,1024]{2,1,0:T(8,128)(2,1)} %copy.136.query, bf16[8,272,1024]{2,1,0:T(8,128)(2,1)} %copy-done.32, bf16[2,128,1024]{2,1,0:T(8,128)(2,1)} %bitcast.333), custom_call_target="tpu_custom_call" | custom-call | flops 8053063680 | bytes 11010048 | tf_op jit(solution)/shard_map/pallas_call | solution.py:273
  354.4 8.0 %concatenate.71 = bf16[16,2,32,2176]{3,2,0,1:T(8,128)(2,1)} concatenate(bf16[16,2,32,1024]{3,2,0,1:T(8,128)(2,1)} %copy.150, bf16[16,2,32,1024]{3,2,0,1:T(8,128)(2,1)} %copy.151, bf16[16,2,32,32]{3,2,0,1:T(8,128)(2,1)S(1)} %copy.152, bf16[16,2,32,1]{3,2,0,1:T(8,128)(2,1)S(1)} %copy.153, bf16[16,2,32,95]{3,2,0,1:T(8,128)(2,1)S(1)} %broadcast_in_dim.120), dimensions={3} | concatenate | bytes 8912896 | tf_op jit(solution)/shard_map/concatenate | solution.py:584
  365.7 4.5 collective-permute-done.35
  382.7 10.4 %collective-permute-done.28 = bf16[256,1024]{1,0:T(8,128)(2,1)} collective-permute-done((bf16[256,1024]{1,0:T(8,128)(2,1)}, bf16[256,1024]{1,0:T(8,128)(2,1)}, u32[]{:S(2)}, u32[]{:S(2)}) %collective-permute-start.28) | collective-permute-done | bytes 524320 | tf_op jit(solution)/shard_map/ppermute | solution.py:91
  396.3 21.8 %collective-permute-done.36 = bf16[8,32,2176]{2,1,0:T(8,128)(2,1)} collective-permute-done((bf16[8,32,2176]{2,1,0:T(8,128)(2,1)}, bf16[8,32,2176]{2,1,0:T(8,128)(2,1)}, u32[]{:S(2)}, u32[]{:S(2)}) %collective-permute-start.36) | collective-permute-done | bytes 1114144 | tf_op jit(solution)/shard_map/ppermute | solution.py:115
  423.0 6.1 %convolution_convert_fusion.2 = bf16[16,128,1024]{2,1,0:T(8,128)(2,1)} fusion(bf16[16,192,128]{2,1,0:T(8,128)(2,1)S(1)} %fusion.12, bf16[16,192,1024]{2,1,0:T(8,128)(2,1)} %bitcast.298), kind=kOutput, calls=%fused_computation.10 | convolution fusion | flops 807403520 | bytes 11272192 | tf_op jit(solution)/shard_map/bst,bsd->btd/dot_general | solution.py:527
  429.0 5.0 gather_fusion
  441.1 8.8 %collective-permute-done.30 = bf16[256,1024]{1,0:T(8,128)(2,1)S(1)} collective-permute-done((bf16[256,1024]{1,0:T(8,128)(2,1)S(1)}, bf16[256,1024]{1,0:T(8,128)(2,1)S(1)}, u32[]{:S(2)}, u32[]{:S(2)}) %collective-permute-start.30) | collective-permute-done | bytes 524320 | tf_op jit(solution)/shard_map/ppermute | solution.py:91
  461.6 7.2 %collective-permute-done.34 = bf16[256,1024]{1,0:T(8,128)(2,1)S(1)} collective-permute-done((bf16[256,1024]{1,0:T(8,128)(2,1)S(1)}, bf16[256,1024]{1,0:T(8,128)(2,1)S(1)}, u32[]{:S(2)}, u32[]{:S(2)}) %collective-permute-start.34) | collective-permute-done | bytes 524320 | tf_op jit(solution)/shard_map/ppermute | solution.py:98
  503.7 10.5 %collective-permute-done.41 = bf16[8,32,1152]{2,1,0:T(8,128)(2,1)S(1)} collective-permute-done((bf16[8,32,1152]{2,1,0:T(8,128)(2,1)S(1)}, bf16[8,32,1152]{2,1,0:T(8,128)(2,1)S(1)}, u32[]{:S(2)}, u32[]{:S(2)}) %collective-permute-start.41) | collective-permute-done | bytes 589856 | tf_op jit(solution)/shard_map/ppermute | solution.py:115
  517.3 6.2 %collective-permute-done.42 = bf16[4,32,1152]{2,1,0:T(8,128)(2,1)S(1)} collective-permute-done((bf16[4,32,1152]{2,1,0:T(8,128)(2,1)S(1)}, bf16[4,32,1152]{2,1,0:T(8,128)(2,1)S(1)}, u32[]{:S(2)}, u32[]{:S(2)}) %collective-permute-start.42) | collective-permute-done | bytes 294944 | tf_op jit(solution)/shard_map/ppermute | solution.py:115
  536.1 33.4 %reduce-scatter.5.cloned.1.call-done = bf16[256,1024]{1,0:T(8,128)(2,1)} async-done(((bf16[2048,1024]{1,0:T(8,128)(2,1)}), bf16[256,1024]{1,0:T(8,128)(2,1)}) %reduce-scatter.5.cloned.1.call-update) | async-done | bytes 524304 | tf_op jit(solution)/shard_map/reduce_scatter | solution.py:597
  (356 shorter events, 219.6 us)
Async XLA Ops:
  7.2 201.9 %all-gather.4.cloned.1.call-start = ((), (), s32[]{:S(2)}) async-start(), calls=%async_computation.4 | async-start | bytes 5242880 | tf_op jit(solution)/shard_map/all_gather | solution.py:436
  7.9 201.1 %all-gather.6.cloned.1.call-start = ((), (), s32[]{:S(2)}) async-start(), calls=%async_computation.5 | async-start | bytes 5242880 | tf_op jit(solution)/shard_map/all_gather | solution.py:437
  8.7 200.4 %all-gather.8.cloned.1.call-start = ((), (), s32[]{:S(2)}) async-start(), calls=%async_computation.6 | async-start | bytes 5242880 | tf_op jit(solution)/shard_map/all_gather | solution.py:438
  22.8 15.9 %collective-permute-start = (bf16[272,1024]{1,0:T(8,128)(2,1)}, bf16[272,1024]{1,0:T(8,128)(2,1)}, u32[]{:S(2)}, u32[]{:S(2)}) collective-permute-start(bf16[272,1024]{1,0:T(8,128)(2,1)} %maximum_maximum_fusion), channel_id=1, source_target_pairs={{0,8},{8,16},{16,24},{24,28},{28,20},{20,12},{12,4},{4,0},{1,9},{9... | collective-permute-start | bytes 1671176 | tf_op jit(solution)/shard_map/ppermute | solution.py:69
  40.4 15.1 %collective-permute-start.4 = (bf16[272,1024]{1,0:T(8,128)(2,1)}, bf16[272,1024]{1,0:T(8,128)(2,1)}, u32[]{:S(2)}, u32[]{:S(2)}) collective-permute-start(bf16[272,1024]{1,0:T(8,128)(2,1)} %maximum_maximum_fusion), channel_id=1, source_target_pairs={{0,4},{8,0},{16,8},{24,16},{28,24},{20,28},{12,20},{4,12},{1,5},{9... | collective-permute-start | bytes 1671176 | tf_op jit(solution)/shard_map/ppermute | solution.py:72
  40.7 473.9 %reduce-scatter.7.cloned.1.call-start = ((), (), s32[]{:S(2)}) async-start(), calls=%async_computation.8 | async-start | bytes 5242880 | tf_op jit(solution)/shard_map/reduce_scatter | solution.py:549
  100.7 14.8 %collective-permute-start.7 = (bf16[256,1024]{1,0:T(8,128)(2,1)S(1)}, bf16[256,1024]{1,0:T(8,128)(2,1)S(1)}, u32[]{:S(2)}, u32[]{:S(2)}) collective-permute-start(bf16[256,1024]{1,0:T(8,128)(2,1)S(1)} %get-tuple-element.41), channel_id=1, source_target_pairs={{0,8},{8,16},{16,24},{24,28},{28,20},{20,12},{12,4},{4,0},{1,9},{9... | collective-permute-start | bytes 1572872 | tf_op jit(solution)/shard_map/ppermute | solution.py:69
  102.3 24.5 %collective-permute-start.14 = (bf16[256,1024]{1,0:T(8,128)(2,1)}, bf16[256,1024]{1,0:T(8,128)(2,1)}, u32[]{:S(2)}, u32[]{:S(2)}) collective-permute-start(bf16[256,1024]{1,0:T(8,128)(2,1)} %bitcast.18), channel_id=1, source_target_pairs={{0,8},{8,16},{16,24},{24,28},{28,20},{20,12},{12,4},{4,0},{1,9},{9... | collective-permute-start | bytes 1572872 | tf_op jit(solution)/shard_map/ppermute | solution.py:69
  115.5 22.6 %collective-permute-start.8 = (bf16[256,1024]{1,0:T(8,128)(2,1)S(1)}, bf16[256,1024]{1,0:T(8,128)(2,1)}, u32[]{:S(2)}, u32[]{:S(2)}) collective-permute-start(bf16[256,1024]{1,0:T(8,128)(2,1)S(1)} %collective-permute-done.7), channel_id=1, source_target_pairs={{0,8},{8,16},{16,24},{24,28},{28,20},{20,12},{12,4},{4,0},{1,9},{9... | collective-permute-start | bytes 1572872 | tf_op jit(solution)/shard_map/ppermute | solution.py:69
  117.1 22.6 %collective-permute-start.11 = (bf16[256,1024]{1,0:T(8,128)(2,1)S(1)}, bf16[256,1024]{1,0:T(8,128)(2,1)S(1)}, u32[]{:S(2)}, u32[]{:S(2)}) collective-permute-start(bf16[256,1024]{1,0:T(8,128)(2,1)S(1)} %get-tuple-element.41), channel_id=1, source_target_pairs={{0,4},{8,0},{16,8},{24,16},{28,24},{20,28},{12,20},{4,12},{1,5},{9... | collective-permute-start | bytes 1572872 | tf_op jit(solution)/shard_map/ppermute | solution.py:72
  117.5 22.7 %collective-permute-start.18 = (bf16[256,1024]{1,0:T(8,128)(2,1)}, bf16[256,1024]{1,0:T(8,128)(2,1)S(1)}, u32[]{:S(2)}, u32[]{:S(2)}) collective-permute-start(bf16[256,1024]{1,0:T(8,128)(2,1)} %bitcast.18), channel_id=1, source_target_pairs={{0,4},{8,0},{16,8},{24,16},{28,24},{20,28},{12,20},{4,12},{1,5},{9... | collective-permute-start | bytes 1572872 | tf_op jit(solution)/shard_map/ppermute | solution.py:72
  126.8 22.4 %collective-permute-start.15 = (bf16[256,1024]{1,0:T(8,128)(2,1)}, bf16[256,1024]{1,0:T(8,128)(2,1)S(1)}, u32[]{:S(2)}, u32[]{:S(2)}) collective-permute-start(bf16[256,1024]{1,0:T(8,128)(2,1)} %collective-permute-done.14), channel_id=1, source_target_pairs={{0,8},{8,16},{16,24},{24,28},{28,20},{20,12},{12,4},{4,0},{1,9},{9... | collective-permute-start | bytes 1572872 | tf_op jit(solution)/shard_map/ppermute | solution.py:69
  138.1 22.4 %collective-permute-start.9 = (bf16[256,1024]{1,0:T(8,128)(2,1)}, bf16[256,1024]{1,0:T(8,128)(2,1)S(1)}, u32[]{:S(2)}, u32[]{:S(2)}) collective-permute-start(bf16[256,1024]{1,0:T(8,128)(2,1)} %collective-permute-done.8), channel_id=1, source_target_pairs={{0,8},{8,16},{16,24},{24,28},{28,20},{20,12},{12,4},{4,0},{1,9},{9... | collective-permute-start | bytes 1572872 | tf_op jit(solution)/shard_map/ppermute | solution.py:69
  139.7 24.2 %collective-permute-start.12 = (bf16[256,1024]{1,0:T(8,128)(2,1)S(1)}, bf16[256,1024]{1,0:T(8,128)(2,1)S(1)}, u32[]{:S(2)}, u32[]{:S(2)}) collective-permute-start(bf16[256,1024]{1,0:T(8,128)(2,1)S(1)} %collective-permute-done.11), channel_id=1, source_target_pairs={{0,4},{8,0},{16,8},{24,16},{28,24},{20,28},{12,20},{4,12},{1,5},{9... | collective-permute-start | bytes 1572872 | tf_op jit(solution)/shard_map/ppermute | solution.py:72
  140.2 26.0 %collective-permute-start.19 = (bf16[256,1024]{1,0:T(8,128)(2,1)S(1)}, bf16[256,1024]{1,0:T(8,128)(2,1)S(1)}, u32[]{:S(2)}, u32[]{:S(2)}) collective-permute-start(bf16[256,1024]{1,0:T(8,128)(2,1)S(1)} %collective-permute-done.18), channel_id=1, source_target_pairs={{0,4},{8,0},{16,8},{24,16},{28,24},{20,28},{12,20},{4,12},{1,5},{9... | collective-permute-start | bytes 1572872 | tf_op jit(solution)/shard_map/ppermute | solution.py:72
  149.2 22.6 %collective-permute-start.16 = (bf16[256,1024]{1,0:T(8,128)(2,1)S(1)}, bf16[256,1024]{1,0:T(8,128)(2,1)}, u32[]{:S(2)}, u32[]{:S(2)}) collective-permute-start(bf16[256,1024]{1,0:T(8,128)(2,1)S(1)} %collective-permute-done.15), channel_id=1, source_target_pairs={{0,8},{8,16},{16,24},{24,28},{28,20},{20,12},{12,4},{4,0},{1,9},{9... | collective-permute-start | bytes 1572872 | tf_op jit(solution)/shard_map/ppermute | solution.py:69
  160.4 22.5 %collective-permute-start.10 = (bf16[256,1024]{1,0:T(8,128)(2,1)S(1)}, bf16[256,1024]{1,0:T(8,128)(2,1)S(1)}, u32[]{:S(2)}, u32[]{:S(2)}) collective-permute-start(bf16[256,1024]{1,0:T(8,128)(2,1)S(1)} %collective-permute-done.9), channel_id=1, source_target_pairs={{0,8},{8,16},{16,24},{24,28},{28,20},{20,12},{12,4},{4,0},{1,9},{9... | collective-permute-start | bytes 1572872 | tf_op jit(solution)/shard_map/ppermute | solution.py:69
  163.9 19.8 %collective-permute-start.13 = (bf16[256,1024]{1,0:T(8,128)(2,1)S(1)}, bf16[256,1024]{1,0:T(8,128)(2,1)S(1)}, u32[]{:S(2)}, u32[]{:S(2)}) collective-permute-start(bf16[256,1024]{1,0:T(8,128)(2,1)S(1)} %collective-permute-done.12), channel_id=1, source_target_pairs={{0,4},{8,0},{16,8},{24,16},{28,24},{20,28},{12,20},{4,12},{1,5},{9... | collective-permute-start | bytes 1572872 | tf_op jit(solution)/shard_map/ppermute | solution.py:72
  166.2 28.2 %collective-permute-start.20 = (bf16[256,1024]{1,0:T(8,128)(2,1)S(1)}, bf16[256,1024]{1,0:T(8,128)(2,1)}, u32[]{:S(2)}, u32[]{:S(2)}) collective-permute-start(bf16[256,1024]{1,0:T(8,128)(2,1)S(1)} %collective-permute-done.19), channel_id=1, source_target_pairs={{0,4},{8,0},{16,8},{24,16},{28,24},{20,28},{12,20},{4,12},{1,5},{9... | collective-permute-start | bytes 1572872 | tf_op jit(solution)/shard_map/ppermute | solution.py:72
  171.8 20.6 %collective-permute-start.17 = (bf16[256,1024]{1,0:T(8,128)(2,1)}, bf16[256,1024]{1,0:T(8,128)(2,1)}, u32[]{:S(2)}, u32[]{:S(2)}) collective-permute-start(bf16[256,1024]{1,0:T(8,128)(2,1)} %collective-permute-done.16), channel_id=1, source_target_pairs={{0,8},{8,16},{16,24},{24,28},{28,20},{20,12},{12,4},{4,0},{1,9},{9... | collective-permute-start | bytes 1572872 | tf_op jit(solution)/shard_map/ppermute | solution.py:69
  247.2 276.8 %reduce-scatter.9.cloned.1.call-start = ((), (), s32[]{:S(2)}) async-start(), calls=%async_computation.9 | async-start | bytes 5242880 | tf_op jit(solution)/shard_map/reduce_scatter | solution.py:549
  259.7 15.4 %collective-permute-start.25 = (bf16[272,1024]{1,0:T(8,128)(2,1)S(1)}, bf16[272,1024]{1,0:T(8,128)(2,1)S(1)}, u32[]{:S(2)}, u32[]{:S(2)}) collective-permute-start(bf16[272,1024]{1,0:T(8,128)(2,1)S(1)} %get-tuple-element.47), channel_id=1, source_target_pairs={{0,4},{8,0},{16,8},{24,16},{28,24},{20,28},{12,20},{4,12},{1,5},{9... | collective-permute-start | bytes 1671176 | tf_op jit(solution)/shard_map/ppermute | solution.py:96
  260.2 269.9 %reduce-scatter.11.cloned.1.call-start = ((), (), s32[]{:S(2)}) async-start(), calls=%async_computation.10 | async-start | bytes 5242880 | tf_op jit(solution)/shard_map/reduce_scatter | solution.py:549
  289.9 14.9 %collective-permute-start.23 = (bf16[272,1024]{1,0:T(8,128)(2,1)S(1)}, bf16[272,1024]{1,0:T(8,128)(2,1)S(1)}, u32[]{:S(2)}, u32[]{:S(2)}) collective-permute-start(bf16[272,1024]{1,0:T(8,128)(2,1)S(1)} %get-tuple-element.44), channel_id=1, source_target_pairs={{0,8},{8,16},{16,24},{24,28},{28,20},{20,12},{12,4},{4,0},{1,9},{9... | collective-permute-start | bytes 1671176 | tf_op jit(solution)/shard_map/ppermute | solution.py:91
  365.6 204.0 %reduce-scatter.5.cloned.1.call-start = ((), (), s32[]{:S(2)}) async-start(), calls=%async_computation.7 | async-start | bytes 4718592 | tf_op jit(solution)/shard_map/reduce_scatter | solution.py:597
  375.7 42.4 %collective-permute-start.36 = (bf16[8,32,2176]{2,1,0:T(8,128)(2,1)}, bf16[8,32,2176]{2,1,0:T(8,128)(2,1)}, u32[]{:S(2)}, u32[]{:S(2)}) collective-permute-start(bf16[8,32,2176]{2,1,0:T(8,128)(2,1)} %dynamic-slice_bitcast_fusion.1), channel_id=1, source_target_pairs={{0,2},{1,3},{2,0},{3,1},{4,6},{5,7},{6,4},{7,5},{8,10},{9,11},{10,... | collective-permute-start | bytes 3342344 | tf_op jit(solution)/shard_map/ppermute | solution.py:115
  382.4 51.6 %collective-permute-start.32 = (bf16[256,1024]{1,0:T(8,128)(2,1)}, bf16[256,1024]{1,0:T(8,128)(2,1)}, u32[]{:S(2)}, u32[]{:S(2)}) collective-permute-start(bf16[256,1024]{1,0:T(8,128)(2,1)} %get-tuple-element.53), channel_id=1, source_target_pairs={{0,4},{8,0},{16,8},{24,16},{28,24},{20,28},{12,20},{4,12},{1,5},{9... | collective-permute-start | bytes 1572872 | tf_op jit(solution)/shard_map/ppermute | solution.py:96
  394.5 39.5 %collective-permute-start.29 = (bf16[256,1024]{1,0:T(8,128)(2,1)S(1)}, bf16[256,1024]{1,0:T(8,128)(2,1)}, u32[]{:S(2)}, u32[]{:S(2)}) collective-permute-start(bf16[256,1024]{1,0:T(8,128)(2,1)S(1)} %fusion.31), channel_id=1, source_target_pairs={{0,8},{8,16},{16,24},{24,28},{28,20},{20,12},{12,4},{4,0},{1,9},{9... | collective-permute-start | bytes 1572872 | tf_op jit(solution)/shard_map/ppermute | solution.py:91
  421.8 16.4 %collective-permute-start.37 = (bf16[4,32,2176]{2,1,0:T(8,128)(2,1)}, bf16[4,32,2176]{2,1,0:T(8,128)(2,1)}, u32[]{:S(2)}, u32[]{:S(2)}) collective-permute-start(bf16[4,32,2176]{2,1,0:T(8,128)(2,1)} %dynamic-slice_bitcast_fusion.3), channel_id=1, source_target_pairs={{0,4},{4,0},{8,12},{12,8},{16,20},{20,16},{24,28},{28,24},{1,5},{5... | collective-permute-start | bytes 1671176 | tf_op jit(solution)/shard_map/ppermute | solution.py:115
  437.6 14.8 %collective-permute-start.33 = (bf16[256,1024]{1,0:T(8,128)(2,1)S(1)}, bf16[256,1024]{1,0:T(8,128)(2,1)S(1)}, u32[]{:S(2)}, u32[]{:S(2)}) collective-permute-start(bf16[256,1024]{1,0:T(8,128)(2,1)S(1)} %get-tuple-element.51), channel_id=1, source_target_pairs={{0,4},{8,0},{16,8},{24,16},{28,24},{20,28},{12,20},{4,12},{1,5},{9... | collective-permute-start | bytes 1572872 | tf_op jit(solution)/shard_map/ppermute | solution.py:96
  439.6 20.3 %collective-permute-start.38 = (bf16[2,32,2176]{2,1,0:T(8,128)(2,1)S(1)}, bf16[2,32,2176]{2,1,0:T(8,128)(2,1)S(1)}, u32[]{:S(2)}, u32[]{:S(2)}) collective-permute-start(bf16[2,32,2176]{2,1,0:T(8,128)(2,1)S(1)} %dynamic-slice_bitcast_fusion.5), channel_id=1, source_target_pairs={{0,8},{4,12},{8,0},{12,4},{16,24},{20,28},{24,16},{28,20},{1,9},{5... | collective-permute-start | bytes 835592 | tf_op jit(solution)/shard_map/ppermute | solution.py:115
  498.1 16.1 %collective-permute-start.41 = (bf16[8,32,1152]{2,1,0:T(8,128)(2,1)S(1)}, bf16[8,32,1152]{2,1,0:T(8,128)(2,1)S(1)}, u32[]{:S(2)}, u32[]{:S(2)}) collective-permute-start(bf16[8,32,1152]{2,1,0:T(8,128)(2,1)S(1)} %dynamic-slice_bitcast_fusion.2), channel_id=1, source_target_pairs={{0,2},{1,3},{2,0},{3,1},{4,6},{5,7},{6,4},{7,5},{8,10},{9,11},{10,... | collective-permute-start | bytes 1769480 | tf_op jit(solution)/shard_map/ppermute | solution.py:115
  (69 other events, 1185.1 us)
Sparse Core Ops, SparseCore 0:
  9.6 37.7 all-gather.3
  48.9 34.9 all-gather.5
  85.5 34.4 all-gather.7
  247.3 44.8 reduce-scatter.6
  294.6 44.5 reduce-scatter.8
  365.7 60.6 reduce-scatter.10
  480.5 89.0 reduce-scatter.4

commit v2 on v0

--- a/solution.py
+++ b/solution.py
@@ -421,7 +421,6 @@
     my_index = lax.axis_index("ctx")
     order = ring_order(ctx_count)
     place_of = jnp.array([order.index(c) for c in range(ctx_count)], jnp.int32)
-    my_place = place_of[my_index]
     table = [
         [order[(order.index(c) - k) % ctx_count] for k in range(ctx_count)] + [c]
         for c in range(ctx_count)
@@ -545,6 +544,9 @@
     ).reshape(EXPERTS, rows)
     grad_sent = grad_sent[:rows]
     mixed_part = to_tokens(combine, produced)
+    mixture = ring_sum(lambda k, p: mixed_part[k], 1)[0]
+    grad_sent, mixture = lax.optimization_barrier((grad_sent, mixture))
+    layer_out = (resid + mixture).astype(jnp.bfloat16).reshape(SEQ_GRP, SEQ_TOK, D)
     gate_grad, up_grad, down_grad = (
         lax.psum_scatter(local, "wsh", scatter_dimension=0).astype(jnp.float32)
         for local in (gate_local, up_local, down_local)
@@ -575,14 +577,6 @@
     )
     grad_query = rotate(grad_query.reshape(SEQ_GRP, SEQ_TOK, HEADS, HEAD_DIM), local_place, -1.0)
     grad_query = grad_query.astype(jnp.bfloat16).reshape(rows, width_q)
-    mixed_part = jnp.take(mixed_part, (my_place - place_of) % ctx_count, axis=0)
-    mixed_part, grad_whole = lax.optimization_barrier((mixed_part, grad_whole))
-    mixture = lax.psum_scatter(
-        mixed_part.reshape(ctx_count * rows, D), "ctx", scatter_dimension=0, tiled=True
-    )
-    layer_out = (
-        (resid + mixture.astype(jnp.float32)).astype(jnp.bfloat16).reshape(SEQ_GRP, SEQ_TOK, D)
-    )
     kv_grad = ring_sum(lambda k, p: grad_whole[k], 1)[0]
     in_first = lax.dot_general(
         normed, grad_query, (((0,), (0,)), ((), ())), preferred_element_type=jnp.float32

time: 571 us -> 544 us (0.953)
  local copies, waits for them, and re-layouts: 90.5 us -> 73.1 us
  starting transfers between devices: 46.5 us -> 56.4 us
  waiting for transfers between devices: 248 us -> 241 us
  other arithmetic: 47.8 us -> 41.8 us
  matrix products: 43.6 us -> 37.8 us
    ppermute x6 -> x9, waiting for transfers between devices: 16.1 us -> 1.4 us  [ring_sum(): down = lax.ppermute(down, 'ctx', behind)]
    ppermute x8 -> x12, waiting for transfers between devices: 86.4 us -> 99.6 us  [ring_sum(): up = lax.ppermute(up, 'ctx', ahead)]
    ppermute x8 -> x12, starting transfers between devices: 10.5 us -> 16.4 us  [ring_sum(): up = lax.ppermute(up, 'ctx', ahead)]
    unnamed x121 -> x97, local copies, waits for them, and re-layouts: 32.8 us -> 29.2 us
    convert_element_type x14 -> x19, other arithmetic: 12.9 us -> 14.1 us  [add_low(): (left.astype(jnp.float32) + right.astype(jnp.float32)).astype(left.dtype)]
  transfers between devices with their start and end apart: 52 -> 58, of which waited for: 33 -> 34; matrix products, arithmetic and copies ran while one was open for 31% -> 27% of each run, Pallas kernels for 6% -> 6%
where the time goes in v2:
time: 544 us; the launch traced here: 535 us
  waiting for transfers between devices  241 us (44%)
  local copies, waits for them, and re-layouts  73.1 us (13%)
  Pallas kernels  70.3 us (13%)
  starting transfers between devices  56.4 us (10%)
  other arithmetic  41.8 us (8%)
  matrix products  37.8 us (7%)
  between operations  15.6 us (3%)
    ppermute x12, waiting for transfers between devices, ring_sum(): up = lax.ppermute(up, 'ctx', ahead)  99.6 us
    ppermute x12, waiting for transfers between devices, ring_gather(): up = lax.ppermute(up, 'ctx', ahead)  90.9 us
    ppermute x10, waiting for transfers between devices, spread(): sent = lax.ppermute(sent, axis, swap)  45.3 us
    pallas_call x1, Pallas kernels, experts_pass(): pl.pallas_call(expert_kernel, grid=(mine, steps), in_specs=[slot_rows(D),...  38.1 us
    unnamed x97, local copies, waits for them, and re-layouts  29.2 us
    ppermute x12, starting transfers between devices, ring_gather(): up = lax.ppermute(up, 'ctx', ahead)  20.4 us
    pallas_call x1, Pallas kernels, attend_back(): pl.pallas_call(attend_back_kernel, out_shape=(jax.ShapeDtypeStruct(query....  18.8 us
    ppermute x12, starting transfers between devices, ring_sum(): up = lax.ppermute(up, 'ctx', ahead)  16.4 us
  transfers between devices with their start and end apart: 58, of which 34 were waited for; matrix products, arithmetic and copies ran while one was open for 27% of the time, Pallas kernels for 6%

profile of v2, /device:TPU:0, one launch (start us, length us, event | category | flops | bytes accessed | tf_op | source)
XLA Modules:
  0.0 535.5 jit_solution(16410252743821523039)
XLA Ops:
  20.7 12.7 %collective-permute-done = bf16[272,1024]{1,0:T(8,128)(2,1)} collective-permute-done((bf16[272,1024]{1,0:T(8,128)(2,1)S(1)}, bf16[272,1024]{1,0:T(8,128)(2,1)}, u32[]{:S(2)}, u32[]{:S(2)}) %collective-permute-start) | collective-permute-done | bytes 557088 | tf_op jit(solution)/shard_map/ppermute | solution.py:69
  38.1 9.4 %collective-permute-done.1 = bf16[272,1024]{1,0:T(8,128)(2,1)} collective-permute-done((bf16[272,1024]{1,0:T(8,128)(2,1)}, bf16[272,1024]{1,0:T(8,128)(2,1)}, u32[]{:S(2)}, u32[]{:S(2)}) %collective-permute-start.1) | collective-permute-done | bytes 557088 | tf_op jit(solution)/shard_map/ppermute | solution.py:69
  52.2 8.6 %collective-permute-done.2 = bf16[272,1024]{1,0:T(8,128)(2,1)} collective-permute-done((bf16[272,1024]{1,0:T(8,128)(2,1)}, bf16[272,1024]{1,0:T(8,128)(2,1)}, u32[]{:S(2)}, u32[]{:S(2)}) %collective-permute-start.2) | collective-permute-done | bytes 557088 | tf_op jit(solution)/shard_map/ppermute | solution.py:69
  66.1 6.9 %collective-permute-done.3 = bf16[272,1024]{1,0:T(8,128)(2,1)S(1)} collective-permute-done((bf16[272,1024]{1,0:T(8,128)(2,1)}, bf16[272,1024]{1,0:T(8,128)(2,1)S(1)}, u32[]{:S(2)}, u32[]{:S(2)}) %collective-permute-start.3) | collective-permute-done | bytes 557088 | tf_op jit(solution)/shard_map/ppermute | solution.py:69
  78.2 13.4 %shard_map.195 = bf16[2,128,1024]{2,1,0:T(8,128)(2,1)} custom-call(s32[9]{0:T(128)} %fusion.73.owner, bf16[2,128,1024]{2,1,0:T(8,128)(2,1)} %copy.135.query, bf16[8,272,1024]{2,1,0:T(8,128)(2,1)} %copy-done.23), custom_call_target="tpu_custom_call" | custom-call | flops 5368709120 | bytes 5505024 | tf_op jit(solution)/shard_map/pallas_call | solution.py:255
  98.7 11.6 %collective-permute-done.7 = bf16[256,1024]{1,0:T(8,128)(2,1)S(1)} collective-permute-done((bf16[256,1024]{1,0:T(8,128)(2,1)S(1)}, bf16[256,1024]{1,0:T(8,128)(2,1)S(1)}, u32[]{:S(2)}, u32[]{:S(2)}) %collective-permute-start.7) | collective-permute-done | bytes 524320 | tf_op jit(solution)/shard_map/ppermute | solution.py:69
  114.4 7.2 %collective-permute-done.14 = bf16[256,1024]{1,0:T(8,128)(2,1)} collective-permute-done((bf16[256,1024]{1,0:T(8,128)(2,1)S(1)}, bf16[256,1024]{1,0:T(8,128)(2,1)}, u32[]{:S(2)}, u32[]{:S(2)}) %collective-permute-start.14) | collective-permute-done | bytes 524320 | tf_op jit(solution)/shard_map/ppermute | solution.py:69
  123.3 9.6 %collective-permute-done.8 = bf16[256,1024]{1,0:T(8,128)(2,1)} collective-permute-done((bf16[256,1024]{1,0:T(8,128)(2,1)S(1)}, bf16[256,1024]{1,0:T(8,128)(2,1)}, u32[]{:S(2)}, u32[]{:S(2)}) %collective-permute-start.8) | collective-permute-done | bytes 524320 | tf_op jit(solution)/shard_map/ppermute | solution.py:69
  136.0 8.0 %collective-permute-done.15 = bf16[256,1024]{1,0:T(8,128)(2,1)S(1)} collective-permute-done((bf16[256,1024]{1,0:T(8,128)(2,1)}, bf16[256,1024]{1,0:T(8,128)(2,1)S(1)}, u32[]{:S(2)}, u32[]{:S(2)}) %collective-permute-start.15) | collective-permute-done | bytes 524320 | tf_op jit(solution)/shard_map/ppermute | solution.py:69
  148.7 6.6 %collective-permute-done.9 = bf16[256,1024]{1,0:T(8,128)(2,1)S(1)} collective-permute-done((bf16[256,1024]{1,0:T(8,128)(2,1)}, bf16[256,1024]{1,0:T(8,128)(2,1)S(1)}, u32[]{:S(2)}, u32[]{:S(2)}) %collective-permute-start.9) | collective-permute-done | bytes 524320 | tf_op jit(solution)/shard_map/ppermute | solution.py:69
  171.0 6.7 %collective-permute-done.10 = bf16[256,1024]{1,0:T(8,128)(2,1)S(1)} collective-permute-done((bf16[256,1024]{1,0:T(8,128)(2,1)S(1)}, bf16[256,1024]{1,0:T(8,128)(2,1)S(1)}, u32[]{:S(2)}, u32[]{:S(2)}) %collective-permute-start.10) | collective-permute-done | bytes 524320 | tf_op jit(solution)/shard_map/ppermute | solution.py:69
  192.6 6.8 %convolution_convert_fusion = bf16[16,192,1024]{2,1,0:T(8,128)(2,1)} fusion(pred[16,192,128]{2,1,0:T(32,128)(4,1)S(1)} %bitcast_compare_fusion, bf16[16,128,1024]{2,1,0:T(8,128)(2,1)} %bitcast.25), kind=kOutput, calls=%fused_computation.5 | convolution fusion | flops 808452096 | bytes 10878976 | tf_op jit(solution)/shard_map/bst,btd->bsd/dot_general | solution.py:509
  199.4 4.5 convolution_convert_fusion.1
  203.9 38.1 %shard_map.196 = (bf16[16,4,48,1024]{3,2,1,0:T(8,128)(2,1)}, bf16[16,4,48,1024]{3,2,1,0:T(8,128)(2,1)}, f32[16,4,48,1]{3,2,1,0:T(8,128)}, bf16[4,4,1024,128]{3,2...) custom-call(bf16[16,4,48,1024]{3,2,1,0:T(8,128)(2,1)} %bitcast.318, ...), custom_call_target="tpu_custom_call" | custom-call | flops 28991029248 | bytes 50331648 | tf_op jit(solution)/shard_map/pallas_call | solution.py:360
  255.5 8.6 %collective-permute-done.28 = bf16[256,1024]{1,0:T(8,128)(2,1)S(1)} collective-permute-done((bf16[256,1024]{1,0:T(8,128)(2,1)S(1)}, bf16[256,1024]{1,0:T(8,128)(2,1)S(1)}, u32[]{:S(2)}, u32[]{:S(2)}) %collective-permute-start.28) | collective-permute-done | bytes 524320 | tf_op jit(solution)/shard_map/ppermute | solution.py:91
  266.0 10.1 %collective-permute-done.21 = bf16[272,1024]{1,0:T(8,128)(2,1)S(1)} collective-permute-done((bf16[272,1024]{1,0:T(8,128)(2,1)S(1)}, bf16[272,1024]{1,0:T(8,128)(2,1)S(1)}, u32[]{:S(2)}, u32[]{:S(2)}) %collective-permute-start.21) | collective-permute-done | bytes 557088 | tf_op jit(solution)/shard_map/ppermute | solution.py:91
  279.1 8.2 %collective-permute-done.29 = bf16[256,1024]{1,0:T(8,128)(2,1)S(1)} collective-permute-done((bf16[256,1024]{1,0:T(8,128)(2,1)S(1)}, bf16[256,1024]{1,0:T(8,128)(2,1)S(1)}, u32[]{:S(2)}, u32[]{:S(2)}) %collective-permute-start.29) | collective-permute-done | bytes 524320 | tf_op jit(solution)/shard_map/ppermute | solution.py:91
  289.2 10.1 %collective-permute-done.22 = bf16[272,1024]{1,0:T(8,128)(2,1)S(1)} collective-permute-done((bf16[272,1024]{1,0:T(8,128)(2,1)S(1)}, bf16[272,1024]{1,0:T(8,128)(2,1)S(1)}, u32[]{:S(2)}, u32[]{:S(2)}) %collective-permute-start.22) | collective-permute-done | bytes 557088 | tf_op jit(solution)/shard_map/ppermute | solution.py:91
  303.0 7.5 %collective-permute-done.30 = bf16[256,1024]{1,0:T(8,128)(2,1)S(1)} collective-permute-done((bf16[256,1024]{1,0:T(8,128)(2,1)S(1)}, bf16[256,1024]{1,0:T(8,128)(2,1)S(1)}, u32[]{:S(2)}, u32[]{:S(2)}) %collective-permute-start.30) | collective-permute-done | bytes 524320 | tf_op jit(solution)/shard_map/ppermute | solution.py:91
  312.4 10.1 %collective-permute-done.23 = bf16[272,1024]{1,0:T(8,128)(2,1)S(1)} collective-permute-done((bf16[272,1024]{1,0:T(8,128)(2,1)S(1)}, bf16[272,1024]{1,0:T(8,128)(2,1)S(1)}, u32[]{:S(2)}, u32[]{:S(2)}) %collective-permute-start.23) | collective-permute-done | bytes 557088 | tf_op jit(solution)/shard_map/ppermute | solution.py:91
  326.0 5.4 %collective-permute-done.31 = bf16[256,1024]{1,0:T(8,128)(2,1)S(1)} collective-permute-done((bf16[256,1024]{1,0:T(8,128)(2,1)S(1)}, bf16[256,1024]{1,0:T(8,128)(2,1)S(1)}, u32[]{:S(2)}, u32[]{:S(2)}) %collective-permute-start.31) | collective-permute-done | bytes 524320 | tf_op jit(solution)/shard_map/ppermute | solution.py:93
  332.9 4.6 collective-permute-done.24
  350.9 18.8 %shard_map.197 = (f32[2,128,1024]{2,1,0:T(8,128)}, bf16[8,256,1024]{2,1,0:T(8,128)(2,1)}) custom-call(s32[9]{0:T(128)} %fusion.73.owner, bf16[2,128,1024]{2,1,0:T(8,128)(2,1)} %copy.135.query, bf16[8,272,1024]{2,1,0:T(8,128)(2,1)} %copy-done.23, bf16[2,128,1024]{2,1,0:T(8,128)(2,1)} %bitcast.356), custom_call_target="tpu_custom_call" | custom-call | flops 8053063680 | bytes 11010048 | tf_op jit(solution)/shard_map/pallas_call | solution.py:273
  380.1 7.4 %concatenate.71 = bf16[16,2,32,2176]{3,2,0,1:T(8,128)(2,1)} concatenate(bf16[16,2,32,1024]{3,2,0,1:T(8,128)(2,1)} %copy.149, bf16[16,2,32,1024]{3,2,0,1:T(8,128)(2,1)S(1)} %copy.150, bf16[16,2,32,32]{3,2,0,1:T(8,128)(2,1)S(1)} %copy.151, bf16[16,2,32,1]{3,2,0,1:T(8,128)(2,1)} %copy.152, bf16[16,2,32,95]{3,2,0,1:T(8,128)(2,1)} %broadcast_in_dim.118), dimensions={3} | concatenate | bytes 8912896 | tf_op jit(solution)/shard_map/concatenate | solution.py:586
  389.4 4.4 collective-permute-done.42
  403.6 12.0 %collective-permute-done.35 = bf16[256,1024]{1,0:T(8,128)(2,1)} collective-permute-done((bf16[256,1024]{1,0:T(8,128)(2,1)}, bf16[256,1024]{1,0:T(8,128)(2,1)}, u32[]{:S(2)}, u32[]{:S(2)}) %collective-permute-start.35) | collective-permute-done | bytes 524320 | tf_op jit(solution)/shard_map/ppermute | solution.py:91
  419.5 5.2 collective-permute-done.43
  436.8 7.8 %collective-permute-done.44 = bf16[4,32,2176]{2,1,0:T(8,128)(2,1)S(1)} collective-permute-done((bf16[4,32,2176]{2,1,0:T(8,128)(2,1)S(1)}, bf16[4,32,2176]{2,1,0:T(8,128)(2,1)S(1)}, u32[]{:S(2)}, u32[]{:S(2)}) %collective-permute-start.44) | collective-permute-done | bytes 557088 | tf_op jit(solution)/shard_map/ppermute | solution.py:115
  444.9 9.2 %collective-permute-done.37 = bf16[256,1024]{1,0:T(8,128)(2,1)S(1)} collective-permute-done((bf16[256,1024]{1,0:T(8,128)(2,1)S(1)}, bf16[256,1024]{1,0:T(8,128)(2,1)S(1)}, u32[]{:S(2)}, u32[]{:S(2)}) %collective-permute-start.37) | collective-permute-done | bytes 524320 | tf_op jit(solution)/shard_map/ppermute | solution.py:91
  458.4 9.7 %collective-permute-done.38 = bf16[256,1024]{1,0:T(8,128)(2,1)S(1)} collective-permute-done((bf16[256,1024]{1,0:T(8,128)(2,1)S(1)}, bf16[256,1024]{1,0:T(8,128)(2,1)S(1)}, u32[]{:S(2)}, u32[]{:S(2)}) %collective-permute-start.38) | collective-permute-done | bytes 524320 | tf_op jit(solution)/shard_map/ppermute | solution.py:93
  496.9 10.8 %collective-permute-done.48 = bf16[8,32,1152]{2,1,0:T(8,128)(2,1)S(1)} collective-permute-done((bf16[8,32,1152]{2,1,0:T(8,128)(2,1)S(1)}, bf16[8,32,1152]{2,1,0:T(8,128)(2,1)S(1)}, u32[]{:S(2)}, u32[]{:S(2)}) %collective-permute-start.48) | collective-permute-done | bytes 589856 | tf_op jit(solution)/shard_map/ppermute | solution.py:115
  510.8 5.4 %collective-permute-done.49 = bf16[4,32,1152]{2,1,0:T(8,128)(2,1)S(1)} collective-permute-done((bf16[4,32,1152]{2,1,0:T(8,128)(2,1)S(1)}, bf16[4,32,1152]{2,1,0:T(8,128)(2,1)S(1)}, u32[]{:S(2)}, u32[]{:S(2)}) %collective-permute-start.49) | collective-permute-done | bytes 294944 | tf_op jit(solution)/shard_map/ppermute | solution.py:115
  (346 shorter events, 214.8 us)
Async XLA Ops:
  7.2 196.7 %all-gather.4.cloned.1.call-start = ((), (), s32[]{:S(2)}) async-start(), calls=%async_computation.3 | async-start | bytes 5242880 | tf_op jit(solution)/shard_map/all_gather | solution.py:435
  7.9 195.9 %all-gather.6.cloned.1.call-start = ((), (), s32[]{:S(2)}) async-start(), calls=%async_computation.4 | async-start | bytes 5242880 | tf_op jit(solution)/shard_map/all_gather | solution.py:436
  8.7 195.2 %all-gather.8.cloned.1.call-start = ((), (), s32[]{:S(2)}) async-start(), calls=%async_computation.5 | async-start | bytes 5242880 | tf_op jit(solution)/shard_map/all_gather | solution.py:437
  35.4 472.6 %reduce-scatter.8.cloned.1.call-start = ((), (), s32[]{:S(2)}) async-start(), calls=%async_computation.8 | async-start | bytes 5242880 | tf_op jit(solution)/shard_map/reduce_scatter | solution.py:551
  97.1 24.5 %collective-permute-start.14 = (bf16[256,1024]{1,0:T(8,128)(2,1)S(1)}, bf16[256,1024]{1,0:T(8,128)(2,1)}, u32[]{:S(2)}, u32[]{:S(2)}) collective-permute-start(bf16[256,1024]{1,0:T(8,128)(2,1)S(1)} %bitcast.334), channel_id=1, source_target_pairs={{0,8},{8,16},{16,24},{24,28},{28,20},{20,12},{12,4},{4,0},{1,9},{9... | collective-permute-start | bytes 1572872 | tf_op jit(solution)/shard_map/ppermute | solution.py:69
  110.3 22.6 %collective-permute-start.8 = (bf16[256,1024]{1,0:T(8,128)(2,1)S(1)}, bf16[256,1024]{1,0:T(8,128)(2,1)}, u32[]{:S(2)}, u32[]{:S(2)}) collective-permute-start(bf16[256,1024]{1,0:T(8,128)(2,1)S(1)} %collective-permute-done.7), channel_id=1, source_target_pairs={{0,8},{8,16},{16,24},{24,28},{28,20},{20,12},{12,4},{4,0},{1,9},{9... | collective-permute-start | bytes 1572872 | tf_op jit(solution)/shard_map/ppermute | solution.py:69
  111.9 22.6 %collective-permute-start.11 = (bf16[256,1024]{1,0:T(8,128)(2,1)S(1)}, bf16[256,1024]{1,0:T(8,128)(2,1)S(1)}, u32[]{:S(2)}, u32[]{:S(2)}) collective-permute-start(bf16[256,1024]{1,0:T(8,128)(2,1)S(1)} %get-tuple-element.43), channel_id=1, source_target_pairs={{0,4},{8,0},{16,8},{24,16},{28,24},{20,28},{12,20},{4,12},{1,5},{9... | collective-permute-start | bytes 1572872 | tf_op jit(solution)/shard_map/ppermute | solution.py:72
  112.3 22.7 %collective-permute-start.18 = (bf16[256,1024]{1,0:T(8,128)(2,1)S(1)}, bf16[256,1024]{1,0:T(8,128)(2,1)S(1)}, u32[]{:S(2)}, u32[]{:S(2)}) collective-permute-start(bf16[256,1024]{1,0:T(8,128)(2,1)S(1)} %bitcast.335), channel_id=1, source_target_pairs={{0,4},{8,0},{16,8},{24,16},{28,24},{20,28},{12,20},{4,12},{1,5},{9... | collective-permute-start | bytes 1572872 | tf_op jit(solution)/shard_map/ppermute | solution.py:72
  121.6 22.4 %collective-permute-start.15 = (bf16[256,1024]{1,0:T(8,128)(2,1)}, bf16[256,1024]{1,0:T(8,128)(2,1)S(1)}, u32[]{:S(2)}, u32[]{:S(2)}) collective-permute-start(bf16[256,1024]{1,0:T(8,128)(2,1)} %collective-permute-done.14), channel_id=1, source_target_pairs={{0,8},{8,16},{16,24},{24,28},{28,20},{20,12},{12,4},{4,0},{1,9},{9... | collective-permute-start | bytes 1572872 | tf_op jit(solution)/shard_map/ppermute | solution.py:69
  132.9 22.4 %collective-permute-start.9 = (bf16[256,1024]{1,0:T(8,128)(2,1)}, bf16[256,1024]{1,0:T(8,128)(2,1)S(1)}, u32[]{:S(2)}, u32[]{:S(2)}) collective-permute-start(bf16[256,1024]{1,0:T(8,128)(2,1)} %collective-permute-done.8), channel_id=1, source_target_pairs={{0,8},{8,16},{16,24},{24,28},{28,20},{20,12},{12,4},{4,0},{1,9},{9... | collective-permute-start | bytes 1572872 | tf_op jit(solution)/shard_map/ppermute | solution.py:69
  134.5 24.2 %collective-permute-start.12 = (bf16[256,1024]{1,0:T(8,128)(2,1)S(1)}, bf16[256,1024]{1,0:T(8,128)(2,1)S(1)}, u32[]{:S(2)}, u32[]{:S(2)}) collective-permute-start(bf16[256,1024]{1,0:T(8,128)(2,1)S(1)} %collective-permute-done.11), channel_id=1, source_target_pairs={{0,4},{8,0},{16,8},{24,16},{28,24},{20,28},{12,20},{4,12},{1,5},{9... | collective-permute-start | bytes 1572872 | tf_op jit(solution)/shard_map/ppermute | solution.py:72
  135.0 26.1 %collective-permute-start.19 = (bf16[256,1024]{1,0:T(8,128)(2,1)S(1)}, bf16[256,1024]{1,0:T(8,128)(2,1)S(1)}, u32[]{:S(2)}, u32[]{:S(2)}) collective-permute-start(bf16[256,1024]{1,0:T(8,128)(2,1)S(1)} %collective-permute-done.18), channel_id=1, source_target_pairs={{0,4},{8,0},{16,8},{24,16},{28,24},{20,28},{12,20},{4,12},{1,5},{9... | collective-permute-start | bytes 1572872 | tf_op jit(solution)/shard_map/ppermute | solution.py:72
  144.0 22.6 %collective-permute-start.16 = (bf16[256,1024]{1,0:T(8,128)(2,1)S(1)}, bf16[256,1024]{1,0:T(8,128)(2,1)}, u32[]{:S(2)}, u32[]{:S(2)}) collective-permute-start(bf16[256,1024]{1,0:T(8,128)(2,1)S(1)} %collective-permute-done.15), channel_id=1, source_target_pairs={{0,8},{8,16},{16,24},{24,28},{28,20},{20,12},{12,4},{4,0},{1,9},{9... | collective-permute-start | bytes 1572872 | tf_op jit(solution)/shard_map/ppermute | solution.py:69
  155.2 22.5 %collective-permute-start.10 = (bf16[256,1024]{1,0:T(8,128)(2,1)S(1)}, bf16[256,1024]{1,0:T(8,128)(2,1)S(1)}, u32[]{:S(2)}, u32[]{:S(2)}) collective-permute-start(bf16[256,1024]{1,0:T(8,128)(2,1)S(1)} %collective-permute-done.9), channel_id=1, source_target_pairs={{0,8},{8,16},{16,24},{24,28},{28,20},{20,12},{12,4},{4,0},{1,9},{9... | collective-permute-start | bytes 1572872 | tf_op jit(solution)/shard_map/ppermute | solution.py:69
  158.7 19.8 %collective-permute-start.13 = (bf16[256,1024]{1,0:T(8,128)(2,1)S(1)}, bf16[256,1024]{1,0:T(8,128)(2,1)S(1)}, u32[]{:S(2)}, u32[]{:S(2)}) collective-permute-start(bf16[256,1024]{1,0:T(8,128)(2,1)S(1)} %collective-permute-done.12), channel_id=1, source_target_pairs={{0,4},{8,0},{16,8},{24,16},{28,24},{20,28},{12,20},{4,12},{1,5},{9... | collective-permute-start | bytes 1572872 | tf_op jit(solution)/shard_map/ppermute | solution.py:72
  161.1 28.0 %collective-permute-start.20 = (bf16[256,1024]{1,0:T(8,128)(2,1)S(1)}, bf16[256,1024]{1,0:T(8,128)(2,1)}, u32[]{:S(2)}, u32[]{:S(2)}) collective-permute-start(bf16[256,1024]{1,0:T(8,128)(2,1)S(1)} %collective-permute-done.19), channel_id=1, source_target_pairs={{0,4},{8,0},{16,8},{24,16},{28,24},{20,28},{12,20},{4,12},{1,5},{9... | collective-permute-start | bytes 1572872 | tf_op jit(solution)/shard_map/ppermute | solution.py:72
  166.6 20.6 %collective-permute-start.17 = (bf16[256,1024]{1,0:T(8,128)(2,1)}, bf16[256,1024]{1,0:T(8,128)(2,1)}, u32[]{:S(2)}, u32[]{:S(2)}) collective-permute-start(bf16[256,1024]{1,0:T(8,128)(2,1)} %collective-permute-done.16), channel_id=1, source_target_pairs={{0,8},{8,16},{16,24},{24,28},{28,20},{20,12},{12,4},{4,0},{1,9},{9... | collective-permute-start | bytes 1572872 | tf_op jit(solution)/shard_map/ppermute | solution.py:69
  242.0 274.3 %reduce-scatter.6.cloned.1.call-start = ((), (), s32[]{:S(2)}) async-start(), calls=%async_computation.7 | async-start | bytes 5242880 | tf_op jit(solution)/shard_map/reduce_scatter | solution.py:551
  253.0 23.1 %collective-permute-start.21 = (bf16[272,1024]{1,0:T(8,128)(2,1)S(1)}, bf16[272,1024]{1,0:T(8,128)(2,1)S(1)}, u32[]{:S(2)}, u32[]{:S(2)}) collective-permute-start(bf16[272,1024]{1,0:T(8,128)(2,1)S(1)} %get-tuple-element.48), channel_id=1, source_target_pairs={{0,8},{8,16},{16,24},{24,28},{28,20},{20,12},{12,4},{4,0},{1,9},{9... | collective-permute-start | bytes 1671176 | tf_op jit(solution)/shard_map/ppermute | solution.py:91
  254.7 34.5 %collective-permute-start.25 = (bf16[272,1024]{1,0:T(8,128)(2,1)S(1)}, bf16[272,1024]{1,0:T(8,128)(2,1)S(1)}, u32[]{:S(2)}, u32[]{:S(2)}) collective-permute-start(bf16[272,1024]{1,0:T(8,128)(2,1)S(1)} %get-tuple-element.49), channel_id=1, source_target_pairs={{0,4},{8,0},{16,8},{24,16},{28,24},{20,28},{12,20},{4,12},{1,5},{9... | collective-permute-start | bytes 1671176 | tf_op jit(solution)/shard_map/ppermute | solution.py:96
  255.1 22.8 %collective-permute-start.32 = (bf16[256,1024]{1,0:T(8,128)(2,1)S(1)}, bf16[256,1024]{1,0:T(8,128)(2,1)S(1)}, u32[]{:S(2)}, u32[]{:S(2)}) collective-permute-start(bf16[256,1024]{1,0:T(8,128)(2,1)S(1)} %bitcast.354), channel_id=1, source_target_pairs={{0,4},{8,0},{16,8},{24,16},{28,24},{20,28},{12,20},{4,12},{1,5},{9... | collective-permute-start | bytes 1572872 | tf_op jit(solution)/shard_map/ppermute | solution.py:96
  264.4 22.9 %collective-permute-start.29 = (bf16[256,1024]{1,0:T(8,128)(2,1)S(1)}, bf16[256,1024]{1,0:T(8,128)(2,1)S(1)}, u32[]{:S(2)}, u32[]{:S(2)}) collective-permute-start(bf16[256,1024]{1,0:T(8,128)(2,1)S(1)} %fusion.36), channel_id=1, source_target_pairs={{0,8},{8,16},{16,24},{24,28},{28,20},{20,12},{12,4},{4,0},{1,9},{9... | collective-permute-start | bytes 1572872 | tf_op jit(solution)/shard_map/ppermute | solution.py:91
  276.3 23.0 %collective-permute-start.22 = (bf16[272,1024]{1,0:T(8,128)(2,1)S(1)}, bf16[272,1024]{1,0:T(8,128)(2,1)S(1)}, u32[]{:S(2)}, u32[]{:S(2)}) collective-permute-start(bf16[272,1024]{1,0:T(8,128)(2,1)S(1)} %fusion.26), channel_id=1, source_target_pairs={{0,8},{8,16},{16,24},{24,28},{28,20},{20,12},{12,4},{4,0},{1,9},{9... | collective-permute-start | bytes 1671176 | tf_op jit(solution)/shard_map/ppermute | solution.py:91
  278.2 23.6 %collective-permute-start.33 = (bf16[256,1024]{1,0:T(8,128)(2,1)S(1)}, bf16[256,1024]{1,0:T(8,128)(2,1)S(1)}, u32[]{:S(2)}, u32[]{:S(2)}) collective-permute-start(bf16[256,1024]{1,0:T(8,128)(2,1)S(1)} %fusion.33), channel_id=1, source_target_pairs={{0,4},{8,0},{16,8},{24,16},{28,24},{20,28},{12,20},{4,12},{1,5},{9... | collective-permute-start | bytes 1572872 | tf_op jit(solution)/shard_map/ppermute | solution.py:96
  287.6 22.9 %collective-permute-start.30 = (bf16[256,1024]{1,0:T(8,128)(2,1)S(1)}, bf16[256,1024]{1,0:T(8,128)(2,1)S(1)}, u32[]{:S(2)}, u32[]{:S(2)}) collective-permute-start(bf16[256,1024]{1,0:T(8,128)(2,1)S(1)} %fusion.35), channel_id=1, source_target_pairs={{0,8},{8,16},{16,24},{24,28},{28,20},{20,12},{12,4},{4,0},{1,9},{9... | collective-permute-start | bytes 1572872 | tf_op jit(solution)/shard_map/ppermute | solution.py:91
  299.7 22.7 %collective-permute-start.23 = (bf16[272,1024]{1,0:T(8,128)(2,1)S(1)}, bf16[272,1024]{1,0:T(8,128)(2,1)S(1)}, u32[]{:S(2)}, u32[]{:S(2)}) collective-permute-start(bf16[272,1024]{1,0:T(8,128)(2,1)S(1)} %get-tuple-element.46), channel_id=1, source_target_pairs={{0,8},{8,16},{16,24},{24,28},{28,20},{20,12},{12,4},{4,0},{1,9},{9... | collective-permute-start | bytes 1671176 | tf_op jit(solution)/shard_map/ppermute | solution.py:91
  301.3 21.1 %collective-permute-start.26 = (bf16[272,1024]{1,0:T(8,128)(2,1)S(1)}, bf16[272,1024]{1,0:T(8,128)(2,1)S(1)}, u32[]{:S(2)}, u32[]{:S(2)}) collective-permute-start(bf16[272,1024]{1,0:T(8,128)(2,1)S(1)} %get-tuple-element.47), channel_id=1, source_target_pairs={{0,4},{8,0},{16,8},{24,16},{28,24},{20,28},{12,20},{4,12},{1,5},{9... | collective-permute-start | bytes 1671176 | tf_op jit(solution)/shard_map/ppermute | solution.py:96
  302.0 24.0 %collective-permute-start.34 = (bf16[256,1024]{1,0:T(8,128)(2,1)S(1)}, bf16[256,1024]{1,0:T(8,128)(2,1)S(1)}, u32[]{:S(2)}, u32[]{:S(2)}) collective-permute-start(bf16[256,1024]{1,0:T(8,128)(2,1)S(1)} %fusion.32), channel_id=1, source_target_pairs={{0,4},{8,0},{16,8},{24,16},{28,24},{20,28},{12,20},{4,12},{1,5},{9... | collective-permute-start | bytes 1572872 | tf_op jit(solution)/shard_map/ppermute | solution.py:98
  310.7 20.7 %collective-permute-start.31 = (bf16[256,1024]{1,0:T(8,128)(2,1)S(1)}, bf16[256,1024]{1,0:T(8,128)(2,1)S(1)}, u32[]{:S(2)}, u32[]{:S(2)}) collective-permute-start(bf16[256,1024]{1,0:T(8,128)(2,1)S(1)} %fusion.34), channel_id=1, source_target_pairs={{0,8},{8,16},{16,24},{24,28},{28,20},{20,12},{12,4},{4,0},{1,9},{9... | collective-permute-start | bytes 1572872 | tf_op jit(solution)/shard_map/ppermute | solution.py:93
  325.9 195.7 %reduce-scatter.4.cloned.1.call-start = ((), (), s32[]{:S(2)}) async-start(), calls=%async_computation.6 | async-start | bytes 5242880 | tf_op jit(solution)/shard_map/reduce_scatter | solution.py:551
  397.7 26.9 %collective-permute-start.43 = (bf16[8,32,2176]{2,1,0:T(8,128)(2,1)}, bf16[8,32,2176]{2,1,0:T(8,128)(2,1)}, u32[]{:S(2)}, u32[]{:S(2)}) collective-permute-start(bf16[8,32,2176]{2,1,0:T(8,128)(2,1)} %dynamic-slice_bitcast_fusion.1), channel_id=1, source_target_pairs={{0,2},{1,3},{2,0},{3,1},{4,6},{5,7},{6,4},{7,5},{8,10},{9,11},{10,... | collective-permute-start | bytes 3342344 | tf_op jit(solution)/shard_map/ppermute | solution.py:115
  403.1 25.6 %collective-permute-start.39 = (bf16[256,1024]{1,0:T(8,128)(2,1)}, bf16[256,1024]{1,0:T(8,128)(2,1)}, u32[]{:S(2)}, u32[]{:S(2)}) collective-permute-start(bf16[256,1024]{1,0:T(8,128)(2,1)} %get-tuple-element.55), channel_id=1, source_target_pairs={{0,4},{8,0},{16,8},{24,16},{28,24},{20,28},{12,20},{4,12},{1,5},{9... | collective-permute-start | bytes 1572872 | tf_op jit(solution)/shard_map/ppermute | solution.py:96
  (63 other events, 977.1 us)
Sparse Core Ops, SparseCore 0:
  9.6 37.7 all-gather.3
  48.9 34.9 all-gather.5
  85.5 34.4 all-gather.7
  242.1 44.8 reduce-scatter.7
  326.0 44.7 reduce-scatter.5
  428.8 44.9 reduce-scatter.3
